TPU v7x, 128 devices: a whole 4x4x4 slice. The times are simulated.
128 devices in a mesh: mp: 8 (over x, y_hi), fsdp: 16 (over z, y_lo, core).
Axes of the slice: x: 4, y: 4 (y_hi: 2, y_lo: 2; y = y_hi * 2 + y_lo), z: 4, core: 2. Of those that a mesh axis runs over, the one named last changes fastest.
Arguments:
- weights: bfloat16 [8, 4096, 14336], P('mp', None, 'fsdp'), may hold values from -6 to 6
- acts: bfloat16 [8, 1024, 4096], P('mp', 'fsdp'), may hold values from -6 to 6
- cotangent: bfloat16 [8, 1024, 14336], P('mp', 'fsdp'), may hold values from -0.26367188 to 0.26367188
- token_ids: int32 [8, 1024], P('mp', 'fsdp'), may hold values from 0 to 31999, as said below
Outputs:
- merged: bfloat16 [4096, 14336], P('mp', 'fsdp')
Inputs may be any that keep to these rules, and one draw needn't show every extreme that they name: `token_ids`: each calibration sequence of 512 tokens holds live ids of 1 to 31999 first and then padding ids 0, at most 256 of them.
All inputs are finite; a program needn't handle non-finite values.
Results may differ from a plain program's by a relative error of at most 0.001.
Values may be sent and summed in bfloat16 or wider, within the bound.
No kernel may reach another device: no remote copies, remote signals or barrier semaphores. Data moves between devices by JAX's collectives and lax.ppermute only.
A program may use at most 128 MiB of HBM per device.

v0:
```python
import functools

import jax
import jax.numpy as jnp
from jax import lax
from jax.experimental import pallas as pl
from jax.sharding import Mesh
from jax.sharding import PartitionSpec as P

SEQS = 2
damping = 0.1


X, YH, Z, YL, CORE = 4, 2, 4, 2, 2
FS = Z * YL * CORE
CHUNKS = ((0, 384), (384, 256), (640, 256))
RTILE = 256


def transpose_kernel(a_ref, out_ref):
    fs, _, t, r = a_ref.shape
    out_ref[0] = a_ref[:, 0].reshape(fs * t, r).T


def transposed(a):
    fs, m, t, r = a.shape
    return pl.pallas_call(
        transpose_kernel,
        out_shape=jax.ShapeDtypeStruct((m, r, fs * t), a.dtype),
        grid=(m,),
        in_specs=[pl.BlockSpec((fs, 1, t, r), lambda i: (0, i, 0, 0))],
        out_specs=pl.BlockSpec((1, r, fs * t), lambda i: (i, 0, 0)),
        name="transpose_acts",
    )(a)


def sums(a_ref, c_refs, w_refs, at):
    seq = a_ref.shape[2] // SEQS
    width = c_refs[0].shape[1]
    numerator = denominator = None
    for m in range(X):
        fisher = None
        for s in range(SEQS):
            if m < X - 1:
                c = c_refs[m][s * seq:(s + 1) * seq, :]
            else:
                c = c_refs[m + s][...]
            g = jnp.dot(a_ref[m, :, s * seq:(s + 1) * seq], c, preferred_element_type=jnp.float32)
            fisher = g * g if fisher is None else fisher + g * g
        importance = fisher / SEQS + damping
        weighted = importance * w_refs[m][:, at:at + width].astype(jnp.float32)
        numerator = weighted if numerator is None else numerator + weighted
        denominator = importance if denominator is None else denominator + importance
    return numerator, denominator


def partial_kernel(at, a_ref, *refs):
    numerator, denominator = sums(a_ref, refs[:5], refs[5:9], at)
    out_ref = refs[9]
    out_ref[0] = numerator
    out_ref[1] = denominator


def merge_kernel(at, a_ref, *refs):
    numerator, denominator = sums(a_ref, refs[:5], refs[5:9], at)
    other_ref, earlier, out_ref = refs[9], refs[10:-1], refs[-1]
    merged = (numerator + other_ref[0]) / (denominator + other_ref[1])
    column = 0
    for ref in earlier:
        out_ref[:, column:column + ref.shape[1]] = ref[...]
        column += ref.shape[1]
    out_ref[:, column:column + merged.shape[1]] = merged.astype(out_ref.dtype)


def specs(a, cs, ws):
    tokens = a.shape[2]
    return (
        [pl.BlockSpec((X, RTILE, tokens), lambda i: (0, i, 0))]
        + [pl.BlockSpec(c.shape, lambda i: (0, 0)) for c in cs]
        + [pl.BlockSpec((RTILE, w.shape[1]), lambda i: (i, 0)) for w in ws]
    )


def partial_sums(a, cs, ws, at):
    rows, cols = ws[0].shape[0], cs[0].shape[1]
    return pl.pallas_call(
        functools.partial(partial_kernel, at),
        out_shape=jax.ShapeDtypeStruct((2, rows, cols), jnp.float32),
        grid=(rows // RTILE,),
        in_specs=specs(a, cs, ws),
        out_specs=pl.BlockSpec((2, RTILE, cols), lambda i: (0, i, 0)),
        name="partial_sums",
    )(a, *cs, *ws)


def merge(a, cs, ws, at, other, earlier):
    rows, cols = ws[0].shape[0], cs[0].shape[1]
    width = cols + sum(e.shape[1] for e in earlier)
    return pl.pallas_call(
        functools.partial(merge_kernel, at),
        out_shape=jax.ShapeDtypeStruct((rows, width), jnp.bfloat16),
        grid=(rows // RTILE,),
        in_specs=specs(a, cs, ws)
        + [pl.BlockSpec((2, RTILE, cols), lambda i: (0, i, 0))]
        + [pl.BlockSpec((RTILE, e.shape[1]), lambda i: (i, 0)) for e in earlier],
        out_specs=pl.BlockSpec((RTILE, width), lambda i: (i, 0)),
        name="merge",
    )(a, *cs, *ws, other, *earlier)


def send(axis, size, step, value):
    return lax.ppermute(value, axis, [(i, (i + step) % size) for i in range(size)])


def per_device(weights, acts, cotangent, token_ids):
    x = lax.axis_index("x")
    y = lax.axis_index("yh")
    rows = weights.shape[1] // (X * YH)
    cols = weights.shape[2]
    fsdp = ("z", "yl", "c")
    tokens = cotangent.shape[1]

    live = (token_ids[0] > 0).astype(acts.dtype)[:, None]

    def spread(half, piece):
        def at_x(step):
            return (lax.rem(x + step, X) * YH + half) * rows

        return [
            piece(at_x(0)),
            send("x", X, 1, piece(at_x(1))),
            send("x", X, -1, piece(at_x(3))),
            send("x", X, 2, piece(at_x(2))),
        ]

    def acts_piece(base):
        return lax.dynamic_slice_in_dim(acts[0], base, YH * rows, 1) * live

    def gathered(pieces, half):
        cut = lax.dynamic_slice_in_dim(pieces, half * rows, rows, 2)
        return lax.all_gather(cut, fsdp, axis=0, tiled=False)

    def weights_for(half, start, width):
        return spread(half, lambda base: lax.dynamic_slice(weights[0], (base, start), (rows, width)))

    def columns_for(start, width):
        cut = cotangent[0].reshape(tokens, FS, cols)[:, :, start:start + width]
        moved = lax.all_to_all(cut, fsdp, split_axis=1, concat_axis=0, tiled=True)
        return moved.reshape(FS * tokens, width)

    def near(own):
        return own, send("x", X, 1, own), send("x", X, -1, own)

    def far(own, left, right):
        half = own.shape[0] // 2
        far0 = send("x", X, 1, left[:half])
        far1 = send("x", X, -1, right[half:])
        return [own, left, right, far0, far1]

    def partial(n, grads):
        return partial_sums(a_other, grads, wp[n], 0)

    def after(value, arrays):
        return lax.optimization_barrier((value, arrays))[1]

    first, rest = CHUNKS[0], (CHUNKS[1][0], cols - CHUNKS[1][0])
    pieces = jnp.stack(spread(0, acts_piece))
    a_other = gathered(pieces, 1 - y)
    a_own = gathered(pieces, y)
    wp = [weights_for(1 - y, *chunk) for chunk in CHUNKS]
    c0 = columns_for(*first)
    c12 = columns_for(*rest)
    grads = [far(*near(c0))]
    nears = []
    for n, (start, width) in enumerate(CHUNKS[1:], 1):
        at = start - rest[0]
        nears.append(near(c12[:, at:at + width]))

    last = CHUNKS[-1]
    wo = [weights_for(y, 0, last[0]), weights_for(y, *last)]

    a_other = transposed(a_other)
    a_own = transposed(a_own)
    partials = [partial(0, grads[0])]
    for n in (1, 2):
        grads.append(far(*after(partials[0], nears[n - 1])))
    partials += [partial(n, grads[n]) for n in (1, 2)]
    sent = [send("yh", YH, 1, p) for p in partials]
    outs = []
    for n, (start, width) in enumerate(CHUNKS):
        final = n == len(CHUNKS) - 1
        w, at = (wo[1], 0) if final else (wo[0], start)
        outs.append(merge(a_own, grads[n], w, at, sent[n], outs if final else []))
    return outs[-1]


def solution(mesh):
    fine = Mesh(mesh.devices.reshape(X, YH, Z, YL, CORE), ("x", "yh", "z", "yl", "c"))
    mp, fsdp = ("x", "yh"), ("z", "yl", "c")

    return jax.shard_map(
        per_device,
        mesh=fine,
        in_specs=(
            P(mp, None, fsdp),
            P(mp, fsdp, None),
            P(mp, fsdp, None),
            P(mp, fsdp),
        ),
        out_specs=P(mp, fsdp),
        check_vma=False,
    )
```

profile of v0, /device:TPU:0, one launch (start us, length us, event | category | flops | bytes accessed | tf_op | source)
XLA Modules:
  0.0 242.6 jit_solution(10627993406176864279)
XLA Ops:
  10.0 2.7 %collective-permute-start.2 = (bf16[64,1024]{1,0:T(8,128)(2,1)S(1)}, bf16[64,1024]{1,0:T(8,128)(2,1)S(1)}, u32[]{:S(2)}, u32[]{:S(2)}) collective-permute-start(bf16[64,1024]{1,0:T(8,128)(2,1)S(1)} %get-tuple-element.40), channel_id=1, source_target_pairs={{0,64},{32,96},{64,0},{96,32},{1,65},{33,97},{65,1},{97,33},{2,66}... | collective-permute-start | bytes 393224 | tf_op jit(solution)/shard_map/ppermute | solution.py:112
  15.2 3.6 %collective-permute-done.2 = bf16[64,1024]{1,0:T(8,128)(2,1)S(1)} collective-permute-done((bf16[64,1024]{1,0:T(8,128)(2,1)S(1)}, bf16[64,1024]{1,0:T(8,128)(2,1)S(1)}, u32[]{:S(2)}, u32[]{:S(2)}) %collective-permute-start.2) | collective-permute-done | bytes 131104 | tf_op jit(solution)/shard_map/ppermute | solution.py:112
  23.4 6.4 %all-to-all-start = ((bf16[64,16,384]{2,0,1:T(8,128)(2,1)}), bf16[64,16,384]{2,0,1:T(8,128)(2,1)S(1)}, u32[]{:S(2)}, u32[]{:S(2)}) async-start(bf16[64,16,384]{2,0,1:T(8,128)(2,1)} %copy.9), calls=%async_computation | async-start | bytes 1572864 | tf_op jit(solution)/shard_map/all_to_all | solution.py:148
  31.6 18.3 %all-to-all-done = bf16[64,16,384]{2,0,1:T(8,128)(2,1)S(1)} async-done(((bf16[64,16,384]{2,0,1:T(8,128)(2,1)}), bf16[64,16,384]{2,0,1:T(8,128)(2,1)S(1)}, u32[]{:S(2)}, u32[]{:S(2)}) %all-to-all-start) | async-done | bytes 786464 | tf_op jit(solution)/shard_map/all_to_all | solution.py:148
  49.9 4.3 %all-to-all-start.1 = ((bf16[64,16,512]{2,0,1:T(8,128)(2,1)}), bf16[64,16,512]{2,0,1:T(8,128)(2,1)}, u32[]{:S(2)}, u32[]{:S(2)}) async-start(bf16[64,16,512]{2,0,1:T(8,128)(2,1)} %copy.10), calls=%async_computation.1 | async-start | bytes 2097152 | tf_op jit(solution)/shard_map/all_to_all | solution.py:148
  56.5 2.6 %dynamic-slice_bitcast_fusion.4 = (bf16[512,384]{1,0:T(8,128)(2,1)}, bf16[512,384]{1,0:T(8,128)(2,1)}, bf16[512,384]{1,0:T(8,128)(2,1)}, bf16[512,384]{1,0:T(8,128)(2,1)}) fusion(bf16[1,4096,896]{2,1,0:T(8,128)(2,1)} %param.4, s32[]{:T(128)S(6)} %select_n.63, s32[]{:T(128)S(6)} %select_n.62, s32[]{:T(128)S(6)} %select_n.61, s32[]{:T(128)S(6)} %select_n.60), kind=kLoop, calls=%fused_computation.5 | loop fusion | bytes 3145744 | tf_op jit(solution)/shard_map/dynamic_slice | solution.py:144
  59.1 2.4 collective-permute-start.9
  63.0 12.7 %all-to-all-done.1 = bf16[64,16,512]{2,0,1:T(8,128)(2,1)} async-done(((bf16[64,16,512]{2,0,1:T(8,128)(2,1)}), bf16[64,16,512]{2,0,1:T(8,128)(2,1)}, u32[]{:S(2)}, u32[]{:S(2)}) %all-to-all-start.1) | async-done | bytes 1048608 | tf_op jit(solution)/shard_map/all_to_all | solution.py:148
  80.0 4.7 %collective-permute-done.9.refs_8_ = bf16[512,384]{1,0:T(8,128)(2,1)S(1)} collective-permute-done((bf16[512,384]{1,0:T(8,128)(2,1)}, bf16[512,384]{1,0:T(8,128)(2,1)S(1)}, u32[]{:S(2)}, u32[]{:S(2)}) %collective-permute-start.9) | collective-permute-done | bytes 393248 | tf_op jit(solution)/shard_map/ppermute | solution.py:112
  86.8 2.5 %collective-permute-start.6 = (bf16[512,384]{1,0:T(8,128)(2,1)}, bf16[512,384]{1,0:T(8,128)(2,1)S(1)}, u32[]{:S(2)}, u32[]{:S(2)}) collective-permute-start(bf16[512,384]{1,0:T(8,128)(2,1)} %slice.42), channel_id=1, source_target_pairs={{0,96},{32,0},{64,32},{96,64},{1,97},{33,1},{65,33},{97,65},{2,98}... | collective-permute-start | bytes 1179656 | tf_op jit(solution)/shard_map/ppermute | solution.py:112
  93.0 3.7 %dynamic-slice_bitcast_fusion.8 = (bf16[512,256]{1,0:T(8,128)(2,1)}, bf16[512,256]{1,0:T(8,128)(2,1)}, bf16[512,256]{1,0:T(8,128)(2,1)}, bf16[512,256]{1,0:T(8,1...) fusion(bf16[1,4096,896]{2,1,0:T(8,128)(2,1)} %param.4, ...), kind=kLoop, calls=%fused_computation.9 | loop fusion | bytes 6291488 | tf_op jit(solution)/shard_map/dynamic_slice | solution.py:144
  96.7 12.8 %collective-permute-done.7.refs_6_ = bf16[512,384]{1,0:T(8,128)(2,1)} collective-permute-done((bf16[512,384]{1,0:T(8,128)(2,1)}, bf16[512,384]{1,0:T(8,128)(2,1)}, u32[]{:S(2)}, u32[]{:S(2)}) %collective-permute-start.7) | collective-permute-done | bytes 393248 | tf_op jit(solution)/shard_map/ppermute | solution.py:112
  113.6 5.3 %transpose_acts.3.a_ref = bf16[4,512,1024]{2,1,0:T(8,128)(2,1)} custom-call(bf16[16,4,64,512]{3,2,1,0:T(8,128)(2,1)} %bitcast.73), custom_call_target="tpu_custom_call" | custom-call | tf_op jit(solution)/shard_map/transpose_acts/pallas_call | solution.py:27
  120.2 6.6 %partial_sums.3 = f32[2,512,384]{2,1,0:T(8,128)} custom-call(bf16[4,512,1024]{2,1,0:T(8,128)(2,1)} %transpose_acts.3.a_ref, bf16[1024,384]{1,0:T(8,128)(2,1)} %bitcast.70, bf16[1024,384]{1,0:T(8,128)(2,1)} %copy-done.2, bf16[1024,384]{1,0:T(8,128)(2,1)} %copy-done.1, bf16[512,384]{1,0:T(8,128)(2,1)} %collective-permute-done.5.refs_3_, ...), custom_call_target="tpu_custom_call" | custom-call | tf_op jit(solution)/shard_map/partial_sums/pallas_call | solution.py:86
  128.7 5.4 %collective-permute-done.31.refs_8_ = bf16[512,256]{1,0:T(8,128)(2,1)} collective-permute-done((bf16[512,256]{1,0:T(8,128)(2,1)}, bf16[512,256]{1,0:T(8,128)(2,1)}, u32[]{:S(2)}, u32[]{:S(2)}) %collective-permute-start.31) | collective-permute-done | bytes 262176 | tf_op jit(solution)/shard_map/ppermute | solution.py:112
  134.1 4.3 %collective-permute-done.29.refs_6_ = bf16[512,256]{1,0:T(8,128)(2,1)} collective-permute-done((bf16[512,256]{1,0:T(8,128)(2,1)}, bf16[512,256]{1,0:T(8,128)(2,1)}, u32[]{:S(2)}, u32[]{:S(2)}) %collective-permute-start.29) | collective-permute-done | bytes 262176 | tf_op jit(solution)/shard_map/ppermute | solution.py:112
  138.4 3.2 %dynamic-slice_bitcast_fusion = (bf16[512,640]{1,0:T(8,128)(2,1)}, bf16[512,640]{1,0:T(8,128)(2,1)}, bf16[512,640]{1,0:T(8,128)(2,1)}, bf16[512,640]{1,0:T(8,128)(2,1)}) fusion(bf16[1,4096,896]{2,1,0:T(8,128)(2,1)} %param.4, s32[]{:T(128)S(6)} %select_n.67, s32[]{:T(128)S(6)} %select_n.66, s32[]{:T(128)S(6)} %select_n.65, s32[]{:T(128)S(6)} %select_n.64), kind=kLoop, calls=%fused_computation | loop fusion | bytes 5242896 | tf_op jit(solution)/shard_map/dynamic_slice | solution.py:144
  142.7 2.5 %collective-permute-start.19 = (bf16[512,256]{1,0:T(8,128)(2,1)}, bf16[512,256]{1,0:T(8,128)(2,1)S(1)}, u32[]{:S(2)}, u32[]{:S(2)}) collective-permute-start(bf16[512,256]{1,0:T(8,128)(2,1)} %get-tuple-element.20), channel_id=1, source_target_pairs={{0,64},{32,96},{64,0},{96,32},{1,65},{33,97},{65,1},{97,33},{2,66}... | collective-permute-start | bytes 786440 | tf_op jit(solution)/shard_map/ppermute | solution.py:112
  145.2 3.2 %collective-permute-start.18 = (bf16[512,256]{1,0:T(8,128)(2,1)}, bf16[512,256]{1,0:T(8,128)(2,1)S(1)}, u32[]{:S(2)}, u32[]{:S(2)}) collective-permute-start(bf16[512,256]{1,0:T(8,128)(2,1)} %get-tuple-element.21), channel_id=1, source_target_pairs={{0,96},{32,0},{64,32},{96,64},{1,97},{33,1},{65,33},{97,65},{2,98}... | collective-permute-start | bytes 786440 | tf_op jit(solution)/shard_map/ppermute | solution.py:112
  148.4 3.0 %collective-permute-start.24 = (f32[2,512,384]{2,1,0:T(8,128)}, f32[2,512,384]{2,1,0:T(8,128)}, u32[]{:S(2)}, u32[]{:S(2)}) collective-permute-start(f32[2,512,384]{2,1,0:T(8,128)} %partial_sums.3), channel_id=1, source_target_pairs={{0,16},{16,0},{1,17},{17,1},{2,18},{18,2},{3,19},{19,3},{4,20},{20... | collective-permute-start | bytes 4718600 | tf_op jit(solution)/shard_map/ppermute | solution.py:112
  151.4 15.9 %collective-permute-done.27.refs_3_ = bf16[512,256]{1,0:T(8,128)(2,1)S(1)} collective-permute-done((bf16[512,256]{1,0:T(8,128)(2,1)S(1)}, bf16[512,256]{1,0:T(8,128)(2,1)S(1)}, u32[]{:S(2)}, u32[]{:S(2)}) %collective-permute-start.27) | collective-permute-done | bytes 262176 | tf_op jit(solution)/shard_map/ppermute | solution.py:112
  168.9 4.7 %partial_sums.5 = f32[2,512,256]{2,1,0:T(8,128)} custom-call(bf16[4,512,1024]{2,1,0:T(8,128)(2,1)} %transpose_acts.3.a_ref, bf16[1024,256]{1,0:T(8,128)(2,1)} %get-tuple-element.14.refs_0_, bf16[1024,256]{1,0:T(8,128)(2,1)} %collective-permute-done.25.refs_1_, bf16[1024,256]{1,0:T(8,128)(2,1)} %collective-permute-done.26.refs_2_, ...), custom_call_target="tpu_custom_call" | custom-call | tf_op jit(solution)/shard_map/partial_sums/pallas_call | solution.py:86
  173.7 3.2 %collective-permute-start.13 = (bf16[512,256]{1,0:T(8,128)(2,1)}, bf16[512,256]{1,0:T(8,128)(2,1)S(1)}, u32[]{:S(2)}, u32[]{:S(2)}) collective-permute-start(bf16[512,256]{1,0:T(8,128)(2,1)} %slice.36), channel_id=1, source_target_pairs={{0,96},{32,0},{64,32},{96,64},{1,97},{33,1},{65,33},{97,65},{2,98}... | collective-permute-start | bytes 786440 | tf_op jit(solution)/shard_map/ppermute | solution.py:112
  177.0 3.1 %collective-permute-start.32 = (f32[2,512,256]{2,1,0:T(8,128)}, f32[2,512,256]{2,1,0:T(8,128)}, u32[]{:S(2)}, u32[]{:S(2)}) collective-permute-start(f32[2,512,256]{2,1,0:T(8,128)} %partial_sums.5), channel_id=1, source_target_pairs={{0,16},{16,0},{1,17},{17,1},{2,18},{18,2},{3,19},{19,3},{4,20},{20... | collective-permute-start | bytes 3145736 | tf_op jit(solution)/shard_map/ppermute | solution.py:112
  181.1 3.6 %collective-permute-done.12.refs_3_ = bf16[512,256]{1,0:T(8,128)(2,1)S(1)} collective-permute-done((bf16[512,256]{1,0:T(8,128)(2,1)}, bf16[512,256]{1,0:T(8,128)(2,1)S(1)}, u32[]{:S(2)}, u32[]{:S(2)}) %collective-permute-start.12) | collective-permute-done | bytes 262176 | tf_op jit(solution)/shard_map/ppermute | solution.py:112
  185.4 4.7 %partial_sums.4 = f32[2,512,256]{2,1,0:T(8,128)} custom-call(bf16[4,512,1024]{2,1,0:T(8,128)(2,1)} %transpose_acts.3.a_ref, bf16[1024,256]{1,0:T(8,128)(2,1)} %copy-done.3, bf16[1024,256]{1,0:T(8,128)(2,1)} %copy-done.5, bf16[1024,256]{1,0:T(8,128)(2,1)} %copy-done.4, bf16[512,256]{1,0:T(8,128)(2,1)} %copy-done.14, bf16[512,256]{1,0:T(8,128)(2,1)} %copy-done.13, ...), custom_call_target="tpu_custom_call" | custom-call | tf_op jit(solution)/shard_map/partial_sums/pallas_call | solution.py:86
  190.1 3.0 %collective-permute-start.20 = (f32[2,512,256]{2,1,0:T(8,128)}, f32[2,512,256]{2,1,0:T(8,128)S(1)}, u32[]{:S(2)}, u32[]{:S(2)}) collective-permute-start(f32[2,512,256]{2,1,0:T(8,128)} %partial_sums.4), channel_id=1, source_target_pairs={{0,16},{16,0},{1,17},{17,1},{2,18},{18,2},{3,19},{19,3},{4,20},{20... | collective-permute-start | bytes 3145736 | tf_op jit(solution)/shard_map/ppermute | solution.py:112
  195.1 13.3 %collective-permute-done.22.refs_7_ = bf16[512,640]{1,0:T(8,128)(2,1)S(1)} collective-permute-done((bf16[512,640]{1,0:T(8,128)(2,1)}, bf16[512,640]{1,0:T(8,128)(2,1)S(1)}, u32[]{:S(2)}, u32[]{:S(2)}) %collective-permute-start.22) | collective-permute-done | bytes 655392 | tf_op jit(solution)/shard_map/ppermute | solution.py:112
  211.9 5.3 %transpose_acts.2.a_ref = bf16[4,512,1024]{2,1,0:T(8,128)(2,1)} custom-call(bf16[16,4,64,512]{3,2,1,0:T(8,128)(2,1)} %bitcast.72), custom_call_target="tpu_custom_call" | custom-call | tf_op jit(solution)/shard_map/transpose_acts/pallas_call | solution.py:27
  217.1 5.3 %merge.4.refs_11_ = bf16[512,256]{1,0:T(8,128)(2,1)} custom-call(bf16[4,512,1024]{2,1,0:T(8,128)(2,1)} %transpose_acts.2.a_ref, bf16[1024,256]{1,0:T(8,128)(2,1)} %get-tuple-element.14.refs_0_, bf16[1024,256]{1,0:T(8,128)(2,1)} %collective-permute-done.25.refs_1_, bf16[1024,256]{1,0:T(8,128)(2,1)} %collective-permute-done.26.refs_2_, ...), custom_call_target="tpu_custom_call" | custom-call | tf_op jit(solution)/shard_map/merge/pallas_call | solution.py:99
  222.5 6.9 %merge.3.refs_10_ = bf16[512,384]{1,0:T(8,128)(2,1)} custom-call(bf16[4,512,1024]{2,1,0:T(8,128)(2,1)} %transpose_acts.2.a_ref, bf16[1024,384]{1,0:T(8,128)(2,1)} %bitcast.71, bf16[1024,384]{1,0:T(8,128)(2,1)} %copy-done.2, bf16[1024,384]{1,0:T(8,128)(2,1)} %copy-done.1, bf16[512,384]{1,0:T(8,128)(2,1)} %collective-permute-done.5.refs_3_, ...), custom_call_target="tpu_custom_call" | custom-call | tf_op jit(solution)/shard_map/merge/pallas_call | solution.py:99
  230.6 5.2 %merge.5 = bf16[512,896]{1,0:T(8,128)(2,1)} custom-call(bf16[4,512,1024]{2,1,0:T(8,128)(2,1)} %transpose_acts.2.a_ref, bf16[1024,256]{1,0:T(8,128)(2,1)} %copy-done.3, bf16[1024,256]{1,0:T(8,128)(2,1)} %copy-done.5, bf16[1024,256]{1,0:T(8,128)(2,1)} %copy-done.4, bf16[512,256]{1,0:T(8,128)(2,1)} %copy-done.14, bf16[512,256]{1,0:T(8,128)(2,1)} %copy-done.13, ...), custom_call_target="tpu_custom_call" | custom-call | tf_op jit(solution)/shard_map/merge/pallas_call | solution.py:99
  (114 shorter events, 44.6 us)
Async XLA Ops:
  6.5 107.1 %all-gather.7.cloned.1.call-start = ((), (), s32[]{:S(2)}) async-start(), calls=%async_computation.3 | async-start | bytes 4456448 | tf_op jit(solution)/shard_map/all_gather | solution.py:141
  19.7 192.1 %all-gather.5.cloned.1.call-start = ((), (), s32[]{:S(2)}) async-start(), calls=%async_computation.2 | async-start | bytes 4456448 | tf_op jit(solution)/shard_map/all_gather | solution.py:141
  23.4 26.5 %all-to-all-start = ((bf16[64,16,384]{2,0,1:T(8,128)(2,1)}), bf16[64,16,384]{2,0,1:T(8,128)(2,1)S(1)}, u32[]{:S(2)}, u32[]{:S(2)}) async-start(bf16[64,16,384]{2,0,1:T(8,128)(2,1)} %copy.9), calls=%async_computation | async-start | bytes 1572864 | tf_op jit(solution)/shard_map/all_to_all | solution.py:148
  49.9 25.8 %all-to-all-start.1 = ((bf16[64,16,512]{2,0,1:T(8,128)(2,1)}), bf16[64,16,512]{2,0,1:T(8,128)(2,1)}, u32[]{:S(2)}, u32[]{:S(2)}) async-start(bf16[64,16,512]{2,0,1:T(8,128)(2,1)} %copy.10), calls=%async_computation.1 | async-start | bytes 2097152 | tf_op jit(solution)/shard_map/all_to_all | solution.py:148
  54.2 30.9 %collective-permute-start.4 = (bf16[1024,384]{1,0:T(8,128)(2,1)S(1)}, bf16[1024,384]{1,0:T(8,128)(2,1)S(1)}, u32[]{:S(2)}, u32[]{:S(2)}) collective-permute-start(bf16[1024,384]{1,0:T(8,128)(2,1)S(1)} %bitcast.68), channel_id=1, source_target_pairs={{0,96},{32,0},{64,32},{96,64},{1,97},{33,1},{65,33},{97,65},{2,98}... | collective-permute-start | bytes 2359304 | tf_op jit(solution)/shard_map/ppermute | solution.py:112
  56.5 30.3 %collective-permute-start.3 = (bf16[1024,384]{1,0:T(8,128)(2,1)S(1)}, bf16[1024,384]{1,0:T(8,128)(2,1)S(1)}, u32[]{:S(2)}, u32[]{:S(2)}) collective-permute-start(bf16[1024,384]{1,0:T(8,128)(2,1)S(1)} %bitcast.69), channel_id=1, source_target_pairs={{0,32},{32,64},{64,96},{96,0},{1,33},{33,65},{65,97},{97,1},{2,34}... | collective-permute-start | bytes 2359304 | tf_op jit(solution)/shard_map/ppermute | solution.py:112
  59.1 25.6 %collective-permute-start.9 = (bf16[512,384]{1,0:T(8,128)(2,1)}, bf16[512,384]{1,0:T(8,128)(2,1)S(1)}, u32[]{:S(2)}, u32[]{:S(2)}) collective-permute-start(bf16[512,384]{1,0:T(8,128)(2,1)} %get-tuple-element.33), channel_id=1, source_target_pairs={{0,64},{32,96},{64,0},{96,32},{1,65},{33,97},{65,1},{97,33},{2,66}... | collective-permute-start | bytes 1179656 | tf_op jit(solution)/shard_map/ppermute | solution.py:112
  61.5 30.2 %collective-permute-start.8 = (bf16[512,384]{1,0:T(8,128)(2,1)}, bf16[512,384]{1,0:T(8,128)(2,1)}, u32[]{:S(2)}, u32[]{:S(2)}) collective-permute-start(bf16[512,384]{1,0:T(8,128)(2,1)} %get-tuple-element.34), channel_id=1, source_target_pairs={{0,96},{32,0},{64,32},{96,64},{1,97},{33,1},{65,33},{97,65},{2,98}... | collective-permute-start | bytes 1179656 | tf_op jit(solution)/shard_map/ppermute | solution.py:112
  77.7 31.8 %collective-permute-start.26 = (bf16[1024,256]{1,0:T(8,128)(2,1)}, bf16[1024,256]{1,0:T(8,128)(2,1)}, u32[]{:S(2)}, u32[]{:S(2)}) collective-permute-start(bf16[1024,256]{1,0:T(8,128)(2,1)} %get-tuple-element.14.refs_0_), channel_id=1, source_target_pairs={{0,96},{32,0},{64,32},{96,64},{1,97},{33,1},{65,33},{97,65},{2,98}... | collective-permute-start | bytes 1572872 | tf_op jit(solution)/shard_map/ppermute | solution.py:112
  84.7 26.8 %collective-permute-start.25 = (bf16[1024,256]{1,0:T(8,128)(2,1)}, bf16[1024,256]{1,0:T(8,128)(2,1)}, u32[]{:S(2)}, u32[]{:S(2)}) collective-permute-start(bf16[1024,256]{1,0:T(8,128)(2,1)} %get-tuple-element.14.refs_0_), channel_id=1, source_target_pairs={{0,32},{32,64},{64,96},{96,0},{1,33},{33,65},{65,97},{97,1},{2,34}... | collective-permute-start | bytes 1572872 | tf_op jit(solution)/shard_map/ppermute | solution.py:112
  85.2 24.3 %collective-permute-start.7 = (bf16[512,384]{1,0:T(8,128)(2,1)}, bf16[512,384]{1,0:T(8,128)(2,1)}, u32[]{:S(2)}, u32[]{:S(2)}) collective-permute-start(bf16[512,384]{1,0:T(8,128)(2,1)} %get-tuple-element.35), channel_id=1, source_target_pairs={{0,32},{32,64},{64,96},{96,0},{1,33},{33,65},{65,97},{97,1},{2,34}... | collective-permute-start | bytes 1179656 | tf_op jit(solution)/shard_map/ppermute | solution.py:112
  86.8 24.8 %collective-permute-start.6 = (bf16[512,384]{1,0:T(8,128)(2,1)}, bf16[512,384]{1,0:T(8,128)(2,1)S(1)}, u32[]{:S(2)}, u32[]{:S(2)}) collective-permute-start(bf16[512,384]{1,0:T(8,128)(2,1)} %slice.42), channel_id=1, source_target_pairs={{0,96},{32,0},{64,32},{96,64},{1,97},{33,1},{65,33},{97,65},{2,98}... | collective-permute-start | bytes 1179656 | tf_op jit(solution)/shard_map/ppermute | solution.py:112
  91.7 27.2 %collective-permute-start.5 = (bf16[512,384]{1,0:T(8,128)(2,1)}, bf16[512,384]{1,0:T(8,128)(2,1)}, u32[]{:S(2)}, u32[]{:S(2)}) collective-permute-start(bf16[512,384]{1,0:T(8,128)(2,1)} %slice.41), channel_id=1, source_target_pairs={{0,32},{32,64},{64,96},{96,0},{1,33},{33,65},{65,97},{97,1},{2,34}... | collective-permute-start | bytes 1179656 | tf_op jit(solution)/shard_map/ppermute | solution.py:112
  109.5 33.2 %collective-permute-start.11 = (bf16[1024,256]{1,0:T(8,128)(2,1)S(1)}, bf16[1024,256]{1,0:T(8,128)(2,1)S(1)}, u32[]{:S(2)}, u32[]{:S(2)}) collective-permute-start(bf16[1024,256]{1,0:T(8,128)(2,1)S(1)} %get-tuple-element.11.refs_0_), channel_id=1, source_target_pairs={{0,96},{32,0},{64,32},{96,64},{1,97},{33,1},{65,33},{97,65},{2,98}... | collective-permute-start | bytes 1572872 | tf_op jit(solution)/shard_map/ppermute | solution.py:112
  109.5 35.7 %collective-permute-start.10 = (bf16[1024,256]{1,0:T(8,128)(2,1)S(1)}, bf16[1024,256]{1,0:T(8,128)(2,1)S(1)}, u32[]{:S(2)}, u32[]{:S(2)}) collective-permute-start(bf16[1024,256]{1,0:T(8,128)(2,1)S(1)} %get-tuple-element.11.refs_0_), channel_id=1, source_target_pairs={{0,32},{32,64},{64,96},{96,0},{1,33},{33,65},{65,97},{97,1},{2,34}... | collective-permute-start | bytes 1572872 | tf_op jit(solution)/shard_map/ppermute | solution.py:112
  111.5 22.6 %collective-permute-start.31 = (bf16[512,256]{1,0:T(8,128)(2,1)}, bf16[512,256]{1,0:T(8,128)(2,1)}, u32[]{:S(2)}, u32[]{:S(2)}) collective-permute-start(bf16[512,256]{1,0:T(8,128)(2,1)} %get-tuple-element.17), channel_id=1, source_target_pairs={{0,64},{32,96},{64,0},{96,32},{1,65},{33,97},{65,1},{97,33},{2,66}... | collective-permute-start | bytes 786440 | tf_op jit(solution)/shard_map/ppermute | solution.py:112
  111.6 26.8 %collective-permute-start.29 = (bf16[512,256]{1,0:T(8,128)(2,1)}, bf16[512,256]{1,0:T(8,128)(2,1)}, u32[]{:S(2)}, u32[]{:S(2)}) collective-permute-start(bf16[512,256]{1,0:T(8,128)(2,1)} %get-tuple-element.18), channel_id=1, source_target_pairs={{0,32},{32,64},{64,96},{96,0},{1,33},{33,65},{65,97},{97,1},{2,34}... | collective-permute-start | bytes 786440 | tf_op jit(solution)/shard_map/ppermute | solution.py:112
  118.9 22.7 %collective-permute-start.30 = (bf16[512,256]{1,0:T(8,128)(2,1)}, bf16[512,256]{1,0:T(8,128)(2,1)S(1)}, u32[]{:S(2)}, u32[]{:S(2)}) collective-permute-start(bf16[512,256]{1,0:T(8,128)(2,1)} %get-tuple-element.28), channel_id=1, source_target_pairs={{0,96},{32,0},{64,32},{96,64},{1,97},{33,1},{65,33},{97,65},{2,98}... | collective-permute-start | bytes 786440 | tf_op jit(solution)/shard_map/ppermute | solution.py:112
  134.1 14.3 %collective-permute-start.28 = (bf16[512,256]{1,0:T(8,128)(2,1)S(1)}, bf16[512,256]{1,0:T(8,128)(2,1)S(1)}, u32[]{:S(2)}, u32[]{:S(2)}) collective-permute-start(bf16[512,256]{1,0:T(8,128)(2,1)S(1)} %slice.39), channel_id=1, source_target_pairs={{0,96},{32,0},{64,32},{96,64},{1,97},{33,1},{65,33},{97,65},{2,98}... | collective-permute-start | bytes 786440 | tf_op jit(solution)/shard_map/ppermute | solution.py:112
  138.4 29.0 %collective-permute-start.27 = (bf16[512,256]{1,0:T(8,128)(2,1)S(1)}, bf16[512,256]{1,0:T(8,128)(2,1)S(1)}, u32[]{:S(2)}, u32[]{:S(2)}) collective-permute-start(bf16[512,256]{1,0:T(8,128)(2,1)S(1)} %slice.38), channel_id=1, source_target_pairs={{0,32},{32,64},{64,96},{96,0},{1,33},{33,65},{65,97},{97,1},{2,34}... | collective-permute-start | bytes 786440 | tf_op jit(solution)/shard_map/ppermute | solution.py:112
  141.6 51.6 %collective-permute-start.23 = (bf16[512,640]{1,0:T(8,128)(2,1)}, bf16[512,640]{1,0:T(8,128)(2,1)S(1)}, u32[]{:S(2)}, u32[]{:S(2)}) collective-permute-start(bf16[512,640]{1,0:T(8,128)(2,1)} %get-tuple-element.29), channel_id=1, source_target_pairs={{0,64},{32,96},{64,0},{96,32},{1,65},{33,97},{65,1},{97,33},{2,66}... | collective-permute-start | bytes 1966088 | tf_op jit(solution)/shard_map/ppermute | solution.py:112
  142.7 31.0 %collective-permute-start.19 = (bf16[512,256]{1,0:T(8,128)(2,1)}, bf16[512,256]{1,0:T(8,128)(2,1)S(1)}, u32[]{:S(2)}, u32[]{:S(2)}) collective-permute-start(bf16[512,256]{1,0:T(8,128)(2,1)} %get-tuple-element.20), channel_id=1, source_target_pairs={{0,64},{32,96},{64,0},{96,32},{1,65},{33,97},{65,1},{97,33},{2,66}... | collective-permute-start | bytes 786440 | tf_op jit(solution)/shard_map/ppermute | solution.py:112
  145.2 31.7 %collective-permute-start.18 = (bf16[512,256]{1,0:T(8,128)(2,1)}, bf16[512,256]{1,0:T(8,128)(2,1)S(1)}, u32[]{:S(2)}, u32[]{:S(2)}) collective-permute-start(bf16[512,256]{1,0:T(8,128)(2,1)} %get-tuple-element.21), channel_id=1, source_target_pairs={{0,96},{32,0},{64,32},{96,64},{1,97},{33,1},{65,33},{97,65},{2,98}... | collective-permute-start | bytes 786440 | tf_op jit(solution)/shard_map/ppermute | solution.py:112
  148.4 74.0 %collective-permute-start.24 = (f32[2,512,384]{2,1,0:T(8,128)}, f32[2,512,384]{2,1,0:T(8,128)}, u32[]{:S(2)}, u32[]{:S(2)}) collective-permute-start(f32[2,512,384]{2,1,0:T(8,128)} %partial_sums.3), channel_id=1, source_target_pairs={{0,16},{16,0},{1,17},{17,1},{2,18},{18,2},{3,19},{19,3},{4,20},{20... | collective-permute-start | bytes 4718600 | tf_op jit(solution)/shard_map/ppermute | solution.py:112
  167.4 9.6 %collective-permute-start.17 = (bf16[512,256]{1,0:T(8,128)(2,1)}, bf16[512,256]{1,0:T(8,128)(2,1)}, u32[]{:S(2)}, u32[]{:S(2)}) collective-permute-start(bf16[512,256]{1,0:T(8,128)(2,1)} %get-tuple-element.22), channel_id=1, source_target_pairs={{0,32},{32,64},{64,96},{96,0},{1,33},{33,65},{65,97},{97,1},{2,34}... | collective-permute-start | bytes 786440 | tf_op jit(solution)/shard_map/ppermute | solution.py:112
  177.0 33.9 %collective-permute-start.32 = (f32[2,512,256]{2,1,0:T(8,128)}, f32[2,512,256]{2,1,0:T(8,128)}, u32[]{:S(2)}, u32[]{:S(2)}) collective-permute-start(f32[2,512,256]{2,1,0:T(8,128)} %partial_sums.5), channel_id=1, source_target_pairs={{0,16},{16,0},{1,17},{17,1},{2,18},{18,2},{3,19},{19,3},{4,20},{20... | collective-permute-start | bytes 3145736 | tf_op jit(solution)/shard_map/ppermute | solution.py:112
  190.1 39.3 %collective-permute-start.20 = (f32[2,512,256]{2,1,0:T(8,128)}, f32[2,512,256]{2,1,0:T(8,128)S(1)}, u32[]{:S(2)}, u32[]{:S(2)}) collective-permute-start(f32[2,512,256]{2,1,0:T(8,128)} %partial_sums.4), channel_id=1, source_target_pairs={{0,16},{16,0},{1,17},{17,1},{2,18},{18,2},{3,19},{19,3},{4,20},{20... | collective-permute-start | bytes 3145736 | tf_op jit(solution)/shard_map/ppermute | solution.py:112
  193.1 15.3 %collective-permute-start.22 = (bf16[512,640]{1,0:T(8,128)(2,1)}, bf16[512,640]{1,0:T(8,128)(2,1)S(1)}, u32[]{:S(2)}, u32[]{:S(2)}) collective-permute-start(bf16[512,640]{1,0:T(8,128)(2,1)} %get-tuple-element.30), channel_id=1, source_target_pairs={{0,96},{32,0},{64,32},{96,64},{1,97},{33,1},{65,33},{97,65},{2,98}... | collective-permute-start | bytes 1966088 | tf_op jit(solution)/shard_map/ppermute | solution.py:112
  193.2 16.6 %collective-permute-start.21 = (bf16[512,640]{1,0:T(8,128)(2,1)}, bf16[512,640]{1,0:T(8,128)(2,1)S(1)}, u32[]{:S(2)}, u32[]{:S(2)}) collective-permute-start(bf16[512,640]{1,0:T(8,128)(2,1)} %get-tuple-element.31), channel_id=1, source_target_pairs={{0,32},{32,64},{64,96},{96,0},{1,33},{33,65},{65,97},{97,1},{2,34}... | collective-permute-start | bytes 1966088 | tf_op jit(solution)/shard_map/ppermute | solution.py:112
  208.4 21.0 %collective-permute-start.16 = (bf16[512,256]{1,0:T(8,128)(2,1)}, bf16[512,256]{1,0:T(8,128)(2,1)S(1)}, u32[]{:S(2)}, u32[]{:S(2)}) collective-permute-start(bf16[512,256]{1,0:T(8,128)(2,1)} %get-tuple-element.24), channel_id=1, source_target_pairs={{0,64},{32,96},{64,0},{96,32},{1,65},{33,97},{65,1},{97,33},{2,66}... | collective-permute-start | bytes 786440 | tf_op jit(solution)/shard_map/ppermute | solution.py:112
  209.8 19.6 %collective-permute-start.15 = (bf16[512,256]{1,0:T(8,128)(2,1)}, bf16[512,256]{1,0:T(8,128)(2,1)S(1)}, u32[]{:S(2)}, u32[]{:S(2)}) collective-permute-start(bf16[512,256]{1,0:T(8,128)(2,1)} %get-tuple-element.25), channel_id=1, source_target_pairs={{0,96},{32,0},{64,32},{96,64},{1,97},{33,1},{65,33},{97,65},{2,98}... | collective-permute-start | bytes 786440 | tf_op jit(solution)/shard_map/ppermute | solution.py:112
  210.9 18.5 %collective-permute-start.14 = (bf16[512,256]{1,0:T(8,128)(2,1)}, bf16[512,256]{1,0:T(8,128)(2,1)}, u32[]{:S(2)}, u32[]{:S(2)}) collective-permute-start(bf16[512,256]{1,0:T(8,128)(2,1)} %get-tuple-element.26), channel_id=1, source_target_pairs={{0,32},{32,64},{64,96},{96,0},{1,33},{33,65},{65,97},{97,1},{2,34}... | collective-permute-start | bytes 786440 | tf_op jit(solution)/shard_map/ppermute | solution.py:112
  (26 other events, 367.8 us)
Sparse Core Ops, SparseCore 0:
  19.9 57.4 all-gather.6
  79.0 37.0 all-gather.4
where the time goes:
time: 244 us; the launch traced here: 243 us
  waiting for transfers between devices  99.4 us (41%)
  starting transfers between devices  58.7 us (24%)
  Pallas kernels  43.9 us (18%)
  local copies, waits for them, and re-layouts  24 us (10%)
  between operations  13.6 us (6%)
  other arithmetic  2.88 us (1%)
    ppermute x33, waiting for transfers between devices, send(): lax.ppermute(value, axis, [(i, (i + step) % size) for i in range(size)])  67.8 us
    ppermute x33, starting transfers between devices, send(): lax.ppermute(value, axis, [(i, (i + step) % size) for i in range(size)])  47.9 us
    all_to_all x2, waiting for transfers between devices, columns_for(): moved = lax.all_to_all(cut, fsdp, split_axis=1, concat_axis=0, tiled=True)  31 us
    pallas_call x3, Pallas kernels, merge(): pl.pallas_call(functools.partial(merge_kernel, at), out_shape=jax.ShapeDt...  17.4 us
    pallas_call x3, Pallas kernels, partial_sums(): pl.pallas_call(functools.partial(partial_kernel, at), out_shape=jax.Shape...  16 us
    all_to_all x2, starting transfers between devices, columns_for(): moved = lax.all_to_all(cut, fsdp, split_axis=1, concat_axis=0, tiled=True)  10.8 us
    pallas_call x2, Pallas kernels, transposed(): pl.pallas_call(transpose_kernel, out_shape=jax.ShapeDtypeStruct((m, r, fs...  10.5 us
    dynamic_slice x3, local copies, waits for them, and re-layouts, weights_for(): lax.dynamic_slice(weights[0], (base, start), (rows, width))  9.51 us
  transfers between devices with their start and end apart: 37, of which 13 were waited for; matrix products, arithmetic and copies ran while one was open for 9% of the time, Pallas kernels for 16%

commit v1 on v0

v1 whole, which is shorter than its diff:
```python
import functools

import jax
import jax.numpy as jnp
from jax import lax
from jax.experimental import pallas as pl
from jax.experimental.pallas import tpu as pltpu
from jax.sharding import Mesh
from jax.sharding import PartitionSpec as P

SEQS = 2
damping = 0.1


X, YH, Z, YL, CORE = 4, 2, 4, 2, 2
FS = Z * YL * CORE
CHUNKS = ((0, 384), (384, 256), (640, 256))
RTILE = 256


VMEM_LIMIT = 24 * 1024 * 1024


def transpose_kernel(at_ref, *refs):
    blocks, out_ref, rows_ref = refs[:-2], refs[-2], refs[-1]
    models, tokens = blocks[0].shape[:2]
    for m in range(models):
        for n in range(YL):
            yl = lax.rem(at_ref[1] + n, YL)
            for k, step in enumerate((0, 3, 1, 2)):
                z = lax.rem(at_ref[0] + step, Z)
                rows_ref[m, z * YL + yl] = blocks[n * Z + k][m]
        turned = rows_ref[m].reshape(rows_ref.shape[1] * tokens, rows_ref.shape[3])
        out_ref[m] = turned.T


def in_vmem(kernel, here, arrays, out_shape, scratch=()):
    return pl.pallas_call(
        kernel,
        out_shape=out_shape,
        in_specs=[pl.BlockSpec(memory_space=pltpu.SMEM)]
        + [pl.BlockSpec(memory_space=pltpu.VMEM) for _ in arrays],
        out_specs=pl.BlockSpec(memory_space=pltpu.VMEM),
        scratch_shapes=list(scratch),
        compiler_params=pltpu.CompilerParams(vmem_limit_bytes=VMEM_LIMIT),
    )(here, *arrays)


def transposed(here, blocks):
    m, t, r = blocks[0].shape
    dtype = blocks[0].dtype
    return in_vmem(
        transpose_kernel, here, blocks,
        jax.ShapeDtypeStruct((m, r, Z * YL * t), dtype),
        [pltpu.VMEM((m, Z * YL, t, r), dtype)],
    )


def sums(at_ref, a_refs, c_refs, w_refs, at, row, width):
    half = a_refs[0].shape[2] // SEQS
    tile = slice(row, row + RTILE)
    numerator = denominator = None
    for m in range(X):
        fisher = None
        for s in range(SEQS):
            g = None
            for n, a_ref in enumerate(a_refs):
                core = at_ref[2] if n == 0 else 1 - at_ref[2]
                c_ref, k = c_refs[m][s]
                c = c_ref[k, :, core].reshape(half, width)
                a = a_ref[m, tile, s * half:(s + 1) * half]
                part = jnp.dot(a, c, preferred_element_type=jnp.float32)
                g = part if g is None else g + part
            fisher = g * g if fisher is None else fisher + g * g
        importance = fisher / SEQS + damping
        weighted = importance * w_refs[m][tile, at:at + width].astype(jnp.float32)
        numerator = weighted if numerator is None else numerator + weighted
        denominator = importance if denominator is None else denominator + importance
    return numerator, denominator


def compute_kernel(layout, at, merging, at_ref, *refs):
    a_refs, refs = refs[:2], refs[2:]
    count = 1 + max(n for pair in layout for n, _ in pair)
    arrays, refs = refs[:count], refs[count:]
    w_refs, refs = refs[:X], refs[X:]
    c_refs = [[(arrays[n], k) for n, k in pair] for pair in layout]
    width = arrays[0].shape[-1]
    rows = w_refs[0].shape[0]
    out_ref = refs[-1]
    for row in range(0, rows, RTILE):
        tile = slice(row, row + RTILE)
        numerator, denominator = sums(at_ref, a_refs, c_refs, w_refs, at, row, width)
        if not merging:
            out_ref[0, tile] = numerator
            out_ref[1, tile] = denominator
            continue
        other_ref, earlier = refs[0], refs[1:-1]
        merged = (numerator + other_ref[0, tile]) / (denominator + other_ref[1, tile])
        column = 0
        for ref in earlier:
            out_ref[tile, column:column + ref.shape[1]] = ref[tile]
            column += ref.shape[1]
        out_ref[tile, column:column + width] = merged.astype(out_ref.dtype)


def partial_sums(here, a, grads, ws, at):
    layout, cs = grads
    rows, cols = ws[0].shape[0], cs[0].shape[-1]
    return in_vmem(
        functools.partial(compute_kernel, layout, at, False), here, [*a, *cs, *ws],
        jax.ShapeDtypeStruct((2, rows, cols), jnp.float32),
    )


def merge(here, a, grads, ws, at, other, earlier):
    layout, cs = grads
    rows, cols = ws[0].shape[0], cs[0].shape[-1]
    width = cols + sum(e.shape[1] for e in earlier)
    return in_vmem(
        functools.partial(compute_kernel, layout, at, True), here,
        [*a, *cs, *ws, other, *earlier],
        jax.ShapeDtypeStruct((rows, width), jnp.bfloat16),
    )


def send(axis, size, step, value):
    return lax.ppermute(value, axis, [(i, (i + step) % size) for i in range(size)])


def per_device(weights, acts, cotangent, token_ids):
    x = lax.axis_index("x")
    y = lax.axis_index("yh")
    rows = weights.shape[1] // (X * YH)
    cols = weights.shape[2]
    fsdp = ("z", "yl", "c")
    tokens = cotangent.shape[1]

    here = jnp.stack([lax.axis_index("z"), lax.axis_index("yl"), lax.axis_index("c")])
    live = (token_ids[0] > 0).astype(acts.dtype)[:, None]

    def spread(half, piece):
        def at_x(step):
            return (lax.rem(x + step, X) * YH + half) * rows

        return [
            piece(at_x(0)),
            send("x", X, 1, piece(at_x(1))),
            send("x", X, -1, piece(at_x(3))),
            send("x", X, 2, piece(at_x(2))),
        ]

    def acts_piece(base):
        return lax.dynamic_slice_in_dim(acts[0], base, YH * rows, 1) * live

    def gathered(pieces, half):
        cut = lax.dynamic_slice_in_dim(pieces, half * rows, rows, 2)
        blocks = []
        for block in (cut, send("yl", YL, 1, cut)):
            blocks += [
                block, send("z", Z, 1, block), send("z", Z, -1, block), send("z", Z, 2, block)
            ]
        own = transposed(here, blocks)
        return own, send("c", CORE, 1, own)

    def weights_for(half, start, width, source=weights[0]):
        def piece(base):
            return lax.dynamic_slice(source, (base, start), (rows, width))

        return spread(half, piece)

    def columns_for(start, width):
        cut = cotangent[0].reshape(tokens, FS, cols)[:, :, start:start + width]
        moved = lax.all_to_all(cut, fsdp, split_axis=1, concat_axis=0, tiled=True)
        return moved.reshape(SEQS, Z // SEQS * YL, CORE, tokens, width)

    def near(own):
        return own, send("x", X, 1, own), send("x", X, -1, own)

    def far(own, left, right):
        far0 = send("x", X, 1, left[:1])
        far1 = send("x", X, -1, right[1:])
        layout = [[(0, 0), (0, 1)], [(1, 0), (1, 1)], [(2, 0), (2, 1)], [(3, 0), (4, 0)]]
        return layout, [own, left, right, far0, far1]

    def split(own):
        own0, own1 = own[:1], own[1:]
        left0 = send("x", X, 1, own0)
        right1 = send("x", X, -1, own1)
        left1 = send("x", X, 1, own1)
        right0 = send("x", X, -1, own0)
        far0 = send("x", X, 1, left0)
        far1 = send("x", X, -1, right1)
        layout = [[(0, 0), (0, 1)], [(1, 0), (2, 0)], [(3, 0), (4, 0)], [(5, 0), (6, 0)]]
        return layout, [own, left0, left1, right0, right1, far0, far1]

    def partial(n, grads):
        return partial_sums(here, a_other, grads, wp[n], 0)

    def after(value, arrays):
        return lax.optimization_barrier((value, arrays))[1]

    first, rest = CHUNKS[0], (CHUNKS[1][0], cols - CHUNKS[1][0])
    pieces = jnp.stack(spread(0, acts_piece))
    a_other = gathered(pieces, 1 - y)
    a_own = gathered(pieces, y)
    wp = [weights_for(1 - y, *chunk) for chunk in CHUNKS]
    c0 = columns_for(*first)
    c12 = columns_for(*rest)
    grads = [split(c0)]
    nears = []
    for n, (start, width) in enumerate(CHUNKS[1:], 1):
        at = start - rest[0]
        nears.append(near(c12[..., at:at + width]))

    partials = [partial(0, grads[0])]
    nears = after(partials[0], nears)
    late = after(partials[0], weights[0])
    grads += [far(*nears[n - 1]) for n in (1, 2)]
    last = CHUNKS[-1]
    wo = [weights_for(y, 0, last[0], late), weights_for(y, *last, late)]
    partials += [partial(n, grads[n]) for n in (1, 2)]
    sent = [send("yh", YH, 1, p) for p in partials]
    outs = []
    for n, (start, width) in enumerate(CHUNKS):
        final = n == len(CHUNKS) - 1
        w, at = (wo[1], 0) if final else (wo[0], start)
        outs.append(merge(here, a_own, grads[n], w, at, sent[n], outs if final else []))
    return outs[-1]


def solution(mesh):
    fine = Mesh(mesh.devices.reshape(X, YH, Z, YL, CORE), ("x", "yh", "z", "yl", "c"))
    mp, fsdp = ("x", "yh"), ("z", "yl", "c")

    return jax.shard_map(
        per_device,
        mesh=fine,
        in_specs=(
            P(mp, None, fsdp),
            P(mp, fsdp, None),
            P(mp, fsdp, None),
            P(mp, fsdp),
        ),
        out_specs=P(mp, fsdp),
        check_vma=False,
    )
```

time: 244 us -> 253 us (1.037)
  Pallas kernels: 43.9 us -> 28.8 us
  starting transfers between devices: 58.7 us -> 73.6 us
  between operations: 13.6 us -> 0.7 us
  waiting for transfers between devices: 99.4 us -> 111 us
  local copies, waits for them, and re-layouts: 24 us -> 33.5 us
    ppermute x33 -> x51, waiting for transfers between devices: 67.8 us -> 111 us  [send(): lax.ppermute(value, axis, [(i, (i + step) % size) for i in range(size)])]
    all_to_all x2, waiting for transfers between devices: 31 us -> 0.01 us  [columns_for(): moved = lax.all_to_all(cut, fsdp, split_axis=1, concat_axis=0, tiled=True)]
    pallas_call x8, Pallas kernels: 43.9 us -> 28.8 us  [in_vmem(): pl.pallas_call(kernel, out_shape=out_shape, in_specs=[pl.BlockSpec(memory...]
    ppermute x33 -> x51, starting transfers between devices: 47.9 us -> 62.8 us  [send(): lax.ppermute(value, axis, [(i, (i + step) % size) for i in range(size)])]
    unnamed x45 -> x107, local copies, waits for them, and re-layouts: 6.36 us -> 17.7 us
    slice x7 -> x6, local copies, waits for them, and re-layouts: 7.11 us -> 4.93 us  [the longest x2 1.75 us: far(): far1 = send('x', X, -1, right[1:])]
    dynamic_slice x3 -> x4, local copies, waits for them, and re-layouts: 9.51 us -> 8.4 us  [piece(): return lax.dynamic_slice(source, (base, start), (rows, width))]
  transfers between devices with their start and end apart: 37 -> 53, of which waited for: 13 -> 24; matrix products, arithmetic and copies ran while one was open for 9% -> 9% of each run, Pallas kernels for 16% -> 10%
where the time goes in v1:
time: 253 us; the launch traced here: 250 us
  waiting for transfers between devices  111 us (44%)
  starting transfers between devices  73.6 us (29%)
  local copies, waits for them, and re-layouts  33.5 us (13%)
  Pallas kernels  28.8 us (11%)
  other arithmetic  2.97 us (1%)
    ppermute x51, waiting for transfers between devices, send(): lax.ppermute(value, axis, [(i, (i + step) % size) for i in range(size)])  111 us
    ppermute x51, starting transfers between devices, send(): lax.ppermute(value, axis, [(i, (i + step) % size) for i in range(size)])  62.8 us
    pallas_call x8, Pallas kernels, in_vmem(): pl.pallas_call(kernel, out_shape=out_shape, in_specs=[pl.BlockSpec(memory...  28.8 us
    unnamed x107, local copies, waits for them, and re-layouts  17.7 us
    all_to_all x2, starting transfers between devices, columns_for(): moved = lax.all_to_all(cut, fsdp, split_axis=1, concat_axis=0, tiled=True)  10.8 us
    dynamic_slice x4, local copies, waits for them, and re-layouts, piece(): return lax.dynamic_slice(source, (base, start), (rows, width))  8.4 us
  transfers between devices with their start and end apart: 53, of which 24 were waited for; matrix products, arithmetic and copies ran while one was open for 9% of the time, Pallas kernels for 10%

profile of v1, /device:TPU:0, one launch (start us, length us, event | category | flops | bytes accessed | tf_op | source)
XLA Modules:
  0.0 250.1 jit_solution(11005312055144552628)
XLA Ops:
  11.8 6.4 %all-to-all-start = ((bf16[64,16,384]{2,0,1:T(8,128)(2,1)}), bf16[64,16,384]{2,0,1:T(8,128)(2,1)S(1)}, u32[]{:S(2)}, u32[]{:S(2)}) async-start(bf16[64,16,384]{2,0,1:T(8,128)(2,1)} %copy.7), calls=%async_computation | async-start | bytes 1572864 | tf_op jit(solution)/shard_map/all_to_all | solution.py:174
  21.4 3.0 %collective-permute-start.13 = (bf16[4,64,512]{2,1,0:T(8,128)(2,1)S(1)}, bf16[4,64,512]{2,1,0:T(8,128)(2,1)S(1)}, u32[]{:S(2)}, u32[]{:S(2)}) collective-permute-start(bf16[4,64,512]{2,1,0:T(8,128)(2,1)S(1)} %get-tuple-element.46.refs_0_), channel_id=1, source_target_pairs={{0,8},{4,12},{8,0},{12,4},{1,9},{5,13},{9,1},{13,5},{2,10},{6,14},... | collective-permute-start | bytes 786440 | tf_op jit(solution)/shard_map/ppermute | solution.py:128
  26.4 9.0 %collective-permute-done.14.refs_4_ = bf16[4,64,512]{2,1,0:T(8,128)(2,1)S(1)} collective-permute-done((bf16[4,64,512]{2,1,0:T(8,128)(2,1)S(1)}, bf16[4,64,512]{2,1,0:T(8,128)(2,1)S(1)}, u32[]{:S(2)}, u32[]{:S(2)}) %collective-permute-start.14) | collective-permute-done | bytes 262176 | tf_op jit(solution)/shard_map/ppermute | solution.py:128
  35.4 3.0 %collective-permute-start.17 = (bf16[4,64,512]{2,1,0:T(8,128)(2,1)S(1)}, bf16[4,64,512]{2,1,0:T(8,128)(2,1)S(1)}, u32[]{:S(2)}, u32[]{:S(2)}) collective-permute-start(bf16[4,64,512]{2,1,0:T(8,128)(2,1)S(1)} %collective-permute-done.14.refs_4_), channel_id=1, source_target_pairs={{0,8},{4,12},{8,0},{12,4},{1,9},{5,13},{9,1},{13,5},{2,10},{6,14},... | collective-permute-start | bytes 786440 | tf_op jit(solution)/shard_map/ppermute | solution.py:128
  45.5 4.3 %all-to-all-start.1 = ((bf16[64,16,512]{2,0,1:T(8,128)(2,1)}), bf16[64,16,512]{2,0,1:T(8,128)(2,1)}, u32[]{:S(2)}, u32[]{:S(2)}) async-start(bf16[64,16,512]{2,0,1:T(8,128)(2,1)} %copy.8), calls=%async_computation.1 | async-start | bytes 2097152 | tf_op jit(solution)/shard_map/all_to_all | solution.py:174
  51.8 3.1 %collective-permute-start.5 = (bf16[4,64,512]{2,1,0:T(8,128)(2,1)S(1)}, bf16[4,64,512]{2,1,0:T(8,128)(2,1)S(1)}, u32[]{:S(2)}, u32[]{:S(2)}) collective-permute-start(bf16[4,64,512]{2,1,0:T(8,128)(2,1)S(1)} %get-tuple-element.47.refs_0_), channel_id=1, source_target_pairs={{0,8},{4,12},{8,0},{12,4},{1,9},{5,13},{9,1},{13,5},{2,10},{6,14},... | collective-permute-start | bytes 786440 | tf_op jit(solution)/shard_map/ppermute | solution.py:128
  61.3 8.4 %collective-permute-done.6.refs_4_ = bf16[4,64,512]{2,1,0:T(8,128)(2,1)S(1)} collective-permute-done((bf16[4,64,512]{2,1,0:T(8,128)(2,1)S(1)}, bf16[4,64,512]{2,1,0:T(8,128)(2,1)S(1)}, u32[]{:S(2)}, u32[]{:S(2)}) %collective-permute-start.6) | collective-permute-done | bytes 262176 | tf_op jit(solution)/shard_map/ppermute | solution.py:128
  76.6 4.3 %collective-permute-done.3.refs_1_ = bf16[4,64,512]{2,1,0:T(8,128)(2,1)S(1)} collective-permute-done((bf16[4,64,512]{2,1,0:T(8,128)(2,1)S(1)}, bf16[4,64,512]{2,1,0:T(8,128)(2,1)S(1)}, u32[]{:S(2)}, u32[]{:S(2)}) %collective-permute-start.3) | collective-permute-done | bytes 262176 | tf_op jit(solution)/shard_map/ppermute | solution.py:128
  88.8 3.5 %collective-permute-done.9.refs_7_ = bf16[4,64,512]{2,1,0:T(8,128)(2,1)S(1)} collective-permute-done((bf16[4,64,512]{2,1,0:T(8,128)(2,1)S(1)}, bf16[4,64,512]{2,1,0:T(8,128)(2,1)S(1)}, u32[]{:S(2)}, u32[]{:S(2)}) %collective-permute-start.9) | collective-permute-done | bytes 262176 | tf_op jit(solution)/shard_map/ppermute | solution.py:128
  105.2 4.1 %collective-permute-done.22.refs_6_ = bf16[1,4,2,64,384]{4,3,2,1,0:T(8,128)(2,1)} collective-permute-done((bf16[1,4,2,64,384]{4,3,2,1,0:T(8,128)(2,1)}, bf16[1,4,2,64,384]{4,3,2,1,0:T(8,128)(2,1)}, u32[]{:S(2)}, u32[]{:S(2)}) %collective-permute-start.22) | collective-permute-done | bytes 393248 | tf_op jit(solution)/shard_map/ppermute | solution.py:128
  109.2 4.3 %collective-permute-done.20.refs_4_ = bf16[1,4,2,64,384]{4,3,2,1,0:T(8,128)(2,1)} collective-permute-done((bf16[1,4,2,64,384]{4,3,2,1,0:T(8,128)(2,1)}, bf16[1,4,2,64,384]{4,3,2,1,0:T(8,128)(2,1)}, u32[]{:S(2)}, u32[]{:S(2)}) %collective-permute-start.20) | collective-permute-done | bytes 393248 | tf_op jit(solution)/shard_map/ppermute | solution.py:128
  113.7 6.7 %collective-permute-done.31.refs_4_ = bf16[2,4,2,64,256]{4,3,2,1,0:T(8,128)(2,1)S(1)} collective-permute-done((bf16[2,4,2,64,256]{4,3,2,1,0:T(8,128)(2,1)S(1)}, bf16[2,4,2,64,256]{4,3,2,1,0:T(8,128)(2,1)S(1)}, u32[]{:S(2)}, u32[]{:S(2)}) %collective-permute-start.31) | collective-permute-done | bytes 524320 | tf_op jit(solution)/shard_map/ppermute | solution.py:128
  120.4 3.3 %collective-permute-done.30.refs_3_ = bf16[2,4,2,64,256]{4,3,2,1,0:T(8,128)(2,1)S(1)} collective-permute-done((bf16[2,4,2,64,256]{4,3,2,1,0:T(8,128)(2,1)S(1)}, bf16[2,4,2,64,256]{4,3,2,1,0:T(8,128)(2,1)S(1)}, u32[]{:S(2)}, u32[]{:S(2)}) %collective-permute-start.30) | collective-permute-done | bytes 524320 | tf_op jit(solution)/shard_map/ppermute | solution.py:128
  123.7 7.9 %collective-permute-done.29.refs_4_ = bf16[2,4,2,64,256]{4,3,2,1,0:T(8,128)(2,1)S(1)} collective-permute-done((bf16[2,4,2,64,256]{4,3,2,1,0:T(8,128)(2,1)S(1)}, bf16[2,4,2,64,256]{4,3,2,1,0:T(8,128)(2,1)S(1)}, u32[]{:S(2)}, u32[]{:S(2)}) %collective-permute-start.29) | collective-permute-done | bytes 524320 | tf_op jit(solution)/shard_map/ppermute | solution.py:128
  134.5 2.8 %collective-permute-start.49 = (bf16[512,256]{1,0:T(8,128)(2,1)S(1)}, bf16[512,256]{1,0:T(8,128)(2,1)S(1)}, u32[]{:S(2)}, u32[]{:S(2)}) collective-permute-start(bf16[512,256]{1,0:T(8,128)(2,1)S(1)} %get-tuple-element.19), channel_id=1, source_target_pairs={{0,64},{32,96},{64,0},{96,32},{1,65},{33,97},{65,1},{97,33},{2,66}... | collective-permute-start | bytes 786440 | tf_op jit(solution)/shard_map/ppermute | solution.py:128
  141.8 5.3 %shard_map.48 = f32[2,512,384]{2,1,0:T(8,128)S(1)} custom-call(s32[3]{0:T(128)S(1)} %pad_add_fusion.at_ref, bf16[4,512,512]{2,1,0:T(8,128)(2,1)} %shard_map.47.refs_0_, bf16[4,512,512]{2,1,0:T(8,128)(2,1)} %collective-permute-done.18.refs_1_, bf16[2,4,2,64,384]{4,3,2,1,0:T(8,128)(2,1)S(1)} %bitcast.55, ...), custom_call_target="tpu_custom_call" | custom-call | tf_op jit(solution)/shard_map/pallas_call | solution.py:38
  148.4 5.0 %collective-permute-done.28.refs_3_ = bf16[2,4,2,64,256]{4,3,2,1,0:T(8,128)(2,1)S(1)} collective-permute-done((bf16[2,4,2,64,256]{4,3,2,1,0:T(8,128)(2,1)S(1)}, bf16[2,4,2,64,256]{4,3,2,1,0:T(8,128)(2,1)S(1)}, u32[]{:S(2)}, u32[]{:S(2)}) %collective-permute-start.28) | collective-permute-done | bytes 524320 | tf_op jit(solution)/shard_map/ppermute | solution.py:128
  157.3 4.2 %collective-permute-done.39.refs_10_ = bf16[512,256]{1,0:T(8,128)(2,1)S(1)} collective-permute-done((bf16[512,256]{1,0:T(8,128)(2,1)S(1)}, bf16[512,256]{1,0:T(8,128)(2,1)S(1)}, u32[]{:S(2)}, u32[]{:S(2)}) %collective-permute-start.39) | collective-permute-done | bytes 262176 | tf_op jit(solution)/shard_map/ppermute | solution.py:128
  165.5 4.7 %collective-permute-start.43 = (bf16[512,640]{1,0:T(8,128)(2,1)S(1)}, bf16[512,640]{1,0:T(8,128)(2,1)S(1)}, u32[]{:S(2)}, u32[]{:S(2)}) collective-permute-start(bf16[512,640]{1,0:T(8,128)(2,1)S(1)} %get-tuple-element.27), channel_id=1, source_target_pairs={{0,64},{32,96},{64,0},{96,32},{1,65},{33,97},{65,1},{97,33},{2,66}... | collective-permute-start | bytes 1966088 | tf_op jit(solution)/shard_map/ppermute | solution.py:128
  170.2 7.1 %collective-permute-done.46.refs_6_ = bf16[1,4,2,64,256]{4,3,2,1,0:T(8,128)(2,1)} collective-permute-done((bf16[1,4,2,64,256]{4,3,2,1,0:T(8,128)(2,1)}, bf16[1,4,2,64,256]{4,3,2,1,0:T(8,128)(2,1)}, u32[]{:S(2)}, u32[]{:S(2)}) %collective-permute-start.46) | collective-permute-done | bytes 262176 | tf_op jit(solution)/shard_map/ppermute | solution.py:128
  177.3 4.7 %collective-permute-start.44 = (f32[2,512,384]{2,1,0:T(8,128)S(1)}, f32[2,512,384]{2,1,0:T(8,128)S(1)}, u32[]{:S(2)}, u32[]{:S(2)}) collective-permute-start(f32[2,512,384]{2,1,0:T(8,128)S(1)} %copy-done.18), channel_id=1, source_target_pairs={{0,16},{16,0},{1,17},{17,1},{2,18},{18,2},{3,19},{19,3},{4,20},{20... | collective-permute-start | bytes 4718600 | tf_op jit(solution)/shard_map/ppermute | solution.py:128
  182.0 3.8 %collective-permute-start.33 = (bf16[1,4,2,64,256]{4,3,2,1,0:T(8,128)(2,1)S(1)}, bf16[1,4,2,64,256]{4,3,2,1,0:T(8,128)(2,1)S(1)}, u32[]{:S(2)}, u32[]{:S(2)}) collective-permute-start(bf16[1,4,2,64,256]{4,3,2,1,0:T(8,128)(2,1)S(1)} %slice.45), channel_id=1, source_target_pairs={{0,96},{32,0},{64,32},{96,64},{1,97},{33,1},{65,33},{97,65},{2,98}... | collective-permute-start | bytes 786440 | tf_op jit(solution)/shard_map/ppermute | solution.py:128
  185.9 3.8 %shard_map.51 = f32[2,512,256]{2,1,0:T(8,128)S(1)} custom-call(s32[3]{0:T(128)S(1)} %pad_add_fusion.at_ref, bf16[4,512,512]{2,1,0:T(8,128)(2,1)} %shard_map.47.refs_0_, bf16[4,512,512]{2,1,0:T(8,128)(2,1)} %collective-permute-done.18.refs_1_, bf16[2,4,2,64,256]{4,3,2,1,0:T(8,128)(2,1)S(1)} %copy-done.1, bf16[2,4,2,64,256]{4,3,2,1,0:T(8,128)(2,1)S(1)} %copy-done.9, ...), custom_call_target="tpu_custom_call" | custom-call | tf_op jit(solution)/shard_map/pallas_call | solution.py:38
  192.0 5.5 %collective-permute-done.32.refs_5_ = bf16[1,4,2,64,256]{4,3,2,1,0:T(8,128)(2,1)S(1)} collective-permute-done((bf16[1,4,2,64,256]{4,3,2,1,0:T(8,128)(2,1)S(1)}, bf16[1,4,2,64,256]{4,3,2,1,0:T(8,128)(2,1)S(1)}, u32[]{:S(2)}, u32[]{:S(2)}) %collective-permute-start.32) | collective-permute-done | bytes 262176 | tf_op jit(solution)/shard_map/ppermute | solution.py:128
  197.5 3.6 %shard_map.49 = f32[2,512,256]{2,1,0:T(8,128)S(1)} custom-call(s32[3]{0:T(128)S(1)} %pad_add_fusion.at_ref, bf16[4,512,512]{2,1,0:T(8,128)(2,1)} %shard_map.47.refs_0_, bf16[4,512,512]{2,1,0:T(8,128)(2,1)} %collective-permute-done.18.refs_1_, bf16[2,4,2,64,256]{4,3,2,1,0:T(8,128)(2,1)S(1)} %get-tuple-element.12.refs_2_, ...), custom_call_target="tpu_custom_call" | custom-call | tf_op jit(solution)/shard_map/pallas_call | solution.py:38
  201.1 3.0 %collective-permute-start.40 = (f32[2,512,256]{2,1,0:T(8,128)S(1)}, f32[2,512,256]{2,1,0:T(8,128)S(1)}, u32[]{:S(2)}, u32[]{:S(2)}) collective-permute-start(f32[2,512,256]{2,1,0:T(8,128)S(1)} %shard_map.49), channel_id=1, source_target_pairs={{0,16},{16,0},{1,17},{17,1},{2,18},{18,2},{3,19},{19,3},{4,20},{20... | collective-permute-start | bytes 3145736 | tf_op jit(solution)/shard_map/ppermute | solution.py:128
  207.4 12.0 %collective-permute-done.42.refs_11_.refs_9_ = bf16[512,640]{1,0:T(8,128)(2,1)S(1)} collective-permute-done((bf16[512,640]{1,0:T(8,128)(2,1)S(1)}, bf16[512,640]{1,0:T(8,128)(2,1)S(1)}, u32[]{:S(2)}, u32[]{:S(2)}) %collective-permute-start.42) | collective-permute-done | bytes 655392 | tf_op jit(solution)/shard_map/ppermute | solution.py:128
  221.6 12.5 %collective-permute-done.50.refs_11_ = f32[2,512,256]{2,1,0:T(8,128)S(1)} collective-permute-done((f32[2,512,256]{2,1,0:T(8,128)S(1)}, f32[2,512,256]{2,1,0:T(8,128)S(1)}, u32[]{:S(2)}, u32[]{:S(2)}) %collective-permute-start.50) | collective-permute-done | bytes 1048608 | tf_op jit(solution)/shard_map/ppermute | solution.py:128
  234.1 3.6 %collective-permute-start.34 = (bf16[512,256]{1,0:T(8,128)(2,1)S(1)}, bf16[512,256]{1,0:T(8,128)(2,1)S(1)}, u32[]{:S(2)}, u32[]{:S(2)}) collective-permute-start(bf16[512,256]{1,0:T(8,128)(2,1)S(1)} %get-tuple-element.33), channel_id=1, source_target_pairs={{0,32},{32,64},{64,96},{96,0},{1,33},{33,65},{65,97},{97,1},{2,34}... | collective-permute-start | bytes 786440 | tf_op jit(solution)/shard_map/ppermute | solution.py:128
  237.7 3.3 %shard_map.52.refs_13_ = bf16[512,256]{1,0:T(8,128)(2,1)S(1)} custom-call(s32[3]{0:T(128)S(1)} %pad_add_fusion.at_ref, bf16[4,512,512]{2,1,0:T(8,128)(2,1)S(1)} %shard_map.46.refs_0_, bf16[4,512,512]{2,1,0:T(8,128)(2,1)} %collective-permute-done.10.refs_1_, bf16[2,4,2,64,256]{4,3,2,1,0:T(8,128)(2,1)S(1)} %copy-done.1, ...), custom_call_target="tpu_custom_call" | custom-call | tf_op jit(solution)/shard_map/pallas_call | solution.py:38
  241.0 4.9 %shard_map.50.refs_12_ = bf16[512,384]{1,0:T(8,128)(2,1)S(1)} custom-call(s32[3]{0:T(128)S(1)} %pad_add_fusion.at_ref, bf16[4,512,512]{2,1,0:T(8,128)(2,1)S(1)} %shard_map.46.refs_0_, bf16[4,512,512]{2,1,0:T(8,128)(2,1)} %collective-permute-done.10.refs_1_, bf16[2,4,2,64,384]{4,3,2,1,0:T(8,128)(2,1)S(1)} %bitcast.56, ...), custom_call_target="tpu_custom_call" | custom-call | tf_op jit(solution)/shard_map/pallas_call | solution.py:38
  246.0 4.1 %shard_map.53 = bf16[512,896]{1,0:T(8,128)(2,1)} custom-call(s32[3]{0:T(128)S(1)} %pad_add_fusion.at_ref, bf16[4,512,512]{2,1,0:T(8,128)(2,1)S(1)} %shard_map.46.refs_0_, bf16[4,512,512]{2,1,0:T(8,128)(2,1)} %collective-permute-done.10.refs_1_, bf16[2,4,2,64,256]{4,3,2,1,0:T(8,128)(2,1)S(1)} %get-tuple-element.12.refs_2_, ...), custom_call_target="tpu_custom_call" | custom-call | tf_op jit(solution)/shard_map/pallas_call | solution.py:38
  (207 shorter events, 84.1 us)
Async XLA Ops:
  1.8 17.4 %collective-permute-start = (bf16[64,1024]{1,0:T(8,128)(2,1)S(1)}, bf16[64,1024]{1,0:T(8,128)(2,1)S(1)}, u32[]{:S(2)}, u32[]{:S(2)}) collective-permute-start(bf16[64,1024]{1,0:T(8,128)(2,1)S(1)} %get-tuple-element.43), channel_id=1, source_target_pairs={{0,32},{32,64},{64,96},{96,0},{1,33},{33,65},{65,97},{97,1},{2,34}... | collective-permute-start | bytes 393224 | tf_op jit(solution)/shard_map/ppermute | solution.py:128
  11.8 33.7 %all-to-all-start = ((bf16[64,16,384]{2,0,1:T(8,128)(2,1)}), bf16[64,16,384]{2,0,1:T(8,128)(2,1)S(1)}, u32[]{:S(2)}, u32[]{:S(2)}) async-start(bf16[64,16,384]{2,0,1:T(8,128)(2,1)} %copy.7), calls=%async_computation | async-start | bytes 1572864 | tf_op jit(solution)/shard_map/all_to_all | solution.py:174
  21.4 18.2 %collective-permute-start.13 = (bf16[4,64,512]{2,1,0:T(8,128)(2,1)S(1)}, bf16[4,64,512]{2,1,0:T(8,128)(2,1)S(1)}, u32[]{:S(2)}, u32[]{:S(2)}) collective-permute-start(bf16[4,64,512]{2,1,0:T(8,128)(2,1)S(1)} %get-tuple-element.46.refs_0_), channel_id=1, source_target_pairs={{0,8},{4,12},{8,0},{12,4},{1,9},{5,13},{9,1},{13,5},{2,10},{6,14},... | collective-permute-start | bytes 786440 | tf_op jit(solution)/shard_map/ppermute | solution.py:128
  24.4 25.5 %collective-permute-start.12 = (bf16[4,64,512]{2,1,0:T(8,128)(2,1)S(1)}, bf16[4,64,512]{2,1,0:T(8,128)(2,1)S(1)}, u32[]{:S(2)}, u32[]{:S(2)}) collective-permute-start(bf16[4,64,512]{2,1,0:T(8,128)(2,1)S(1)} %get-tuple-element.46.refs_0_), channel_id=1, source_target_pairs={{0,12},{4,0},{8,4},{12,8},{1,13},{5,1},{9,5},{13,9},{2,14},{6,2},{... | collective-permute-start | bytes 786440 | tf_op jit(solution)/shard_map/ppermute | solution.py:128
  25.6 26.2 %collective-permute-start.11 = (bf16[4,64,512]{2,1,0:T(8,128)(2,1)S(1)}, bf16[4,64,512]{2,1,0:T(8,128)(2,1)S(1)}, u32[]{:S(2)}, u32[]{:S(2)}) collective-permute-start(bf16[4,64,512]{2,1,0:T(8,128)(2,1)S(1)} %get-tuple-element.46.refs_0_), channel_id=1, source_target_pairs={{0,4},{4,8},{8,12},{12,0},{1,5},{5,9},{9,13},{13,1},{2,6},{6,10},{... | collective-permute-start | bytes 786440 | tf_op jit(solution)/shard_map/ppermute | solution.py:128
  35.4 19.4 %collective-permute-start.17 = (bf16[4,64,512]{2,1,0:T(8,128)(2,1)S(1)}, bf16[4,64,512]{2,1,0:T(8,128)(2,1)S(1)}, u32[]{:S(2)}, u32[]{:S(2)}) collective-permute-start(bf16[4,64,512]{2,1,0:T(8,128)(2,1)S(1)} %collective-permute-done.14.refs_4_), channel_id=1, source_target_pairs={{0,8},{4,12},{8,0},{12,4},{1,9},{5,13},{9,1},{13,5},{2,10},{6,14},... | collective-permute-start | bytes 786440 | tf_op jit(solution)/shard_map/ppermute | solution.py:128
  38.4 17.6 %collective-permute-start.16 = (bf16[4,64,512]{2,1,0:T(8,128)(2,1)S(1)}, bf16[4,64,512]{2,1,0:T(8,128)(2,1)S(1)}, u32[]{:S(2)}, u32[]{:S(2)}) collective-permute-start(bf16[4,64,512]{2,1,0:T(8,128)(2,1)S(1)} %collective-permute-done.14.refs_4_), channel_id=1, source_target_pairs={{0,12},{4,0},{8,4},{12,8},{1,13},{5,1},{9,5},{13,9},{2,14},{6,2},{... | collective-permute-start | bytes 786440 | tf_op jit(solution)/shard_map/ppermute | solution.py:128
  39.6 16.4 %collective-permute-start.15 = (bf16[4,64,512]{2,1,0:T(8,128)(2,1)S(1)}, bf16[4,64,512]{2,1,0:T(8,128)(2,1)S(1)}, u32[]{:S(2)}, u32[]{:S(2)}) collective-permute-start(bf16[4,64,512]{2,1,0:T(8,128)(2,1)S(1)} %collective-permute-done.14.refs_4_), channel_id=1, source_target_pairs={{0,4},{4,8},{8,12},{12,0},{1,5},{5,9},{9,13},{13,1},{2,6},{6,10},{... | collective-permute-start | bytes 786440 | tf_op jit(solution)/shard_map/ppermute | solution.py:128
  45.5 52.1 %all-to-all-start.1 = ((bf16[64,16,512]{2,0,1:T(8,128)(2,1)}), bf16[64,16,512]{2,0,1:T(8,128)(2,1)}, u32[]{:S(2)}, u32[]{:S(2)}) async-start(bf16[64,16,512]{2,0,1:T(8,128)(2,1)} %copy.8), calls=%async_computation.1 | async-start | bytes 2097152 | tf_op jit(solution)/shard_map/all_to_all | solution.py:174
  49.9 19.8 %collective-permute-start.6 = (bf16[4,64,512]{2,1,0:T(8,128)(2,1)S(1)}, bf16[4,64,512]{2,1,0:T(8,128)(2,1)S(1)}, u32[]{:S(2)}, u32[]{:S(2)}) collective-permute-start(bf16[4,64,512]{2,1,0:T(8,128)(2,1)S(1)} %get-tuple-element.47.refs_0_), channel_id=1, source_target_pairs={{0,2},{2,0},{1,3},{3,1},{4,6},{6,4},{5,7},{7,5},{8,10},{10,8},{9,1... | collective-permute-start | bytes 786440 | tf_op jit(solution)/shard_map/ppermute | solution.py:128
  51.8 19.4 %collective-permute-start.5 = (bf16[4,64,512]{2,1,0:T(8,128)(2,1)S(1)}, bf16[4,64,512]{2,1,0:T(8,128)(2,1)S(1)}, u32[]{:S(2)}, u32[]{:S(2)}) collective-permute-start(bf16[4,64,512]{2,1,0:T(8,128)(2,1)S(1)} %get-tuple-element.47.refs_0_), channel_id=1, source_target_pairs={{0,8},{4,12},{8,0},{12,4},{1,9},{5,13},{9,1},{13,5},{2,10},{6,14},... | collective-permute-start | bytes 786440 | tf_op jit(solution)/shard_map/ppermute | solution.py:128
  54.8 20.4 %collective-permute-start.4 = (bf16[4,64,512]{2,1,0:T(8,128)(2,1)S(1)}, bf16[4,64,512]{2,1,0:T(8,128)(2,1)S(1)}, u32[]{:S(2)}, u32[]{:S(2)}) collective-permute-start(bf16[4,64,512]{2,1,0:T(8,128)(2,1)S(1)} %get-tuple-element.47.refs_0_), channel_id=1, source_target_pairs={{0,12},{4,0},{8,4},{12,8},{1,13},{5,1},{9,5},{13,9},{2,14},{6,2},{... | collective-permute-start | bytes 786440 | tf_op jit(solution)/shard_map/ppermute | solution.py:128
  58.5 81.5 %collective-permute-start.18 = (bf16[4,512,512]{2,1,0:T(8,128)(2,1)}, bf16[4,512,512]{2,1,0:T(8,128)(2,1)}, u32[]{:S(2)}, u32[]{:S(2)}) collective-permute-start(bf16[4,512,512]{2,1,0:T(8,128)(2,1)} %shard_map.47.refs_0_), channel_id=1, source_target_pairs={{0,1},{1,0},{2,3},{3,2},{4,5},{5,4},{6,7},{7,6},{8,9},{9,8},{10,11... | collective-permute-start | bytes 6291464 | tf_op jit(solution)/shard_map/ppermute | solution.py:128
  60.8 21.1 %collective-permute-start.27 = (bf16[512,384]{1,0:T(8,128)(2,1)S(1)}, bf16[512,384]{1,0:T(8,128)(2,1)S(1)}, u32[]{:S(2)}, u32[]{:S(2)}) collective-permute-start(bf16[512,384]{1,0:T(8,128)(2,1)S(1)} %get-tuple-element.35), channel_id=1, source_target_pairs={{0,64},{32,96},{64,0},{96,32},{1,65},{33,97},{65,1},{97,33},{2,66}... | collective-permute-start | bytes 1179656 | tf_op jit(solution)/shard_map/ppermute | solution.py:128
  101.5 18.9 %collective-permute-start.31 = (bf16[2,4,2,64,256]{4,3,2,1,0:T(8,128)(2,1)S(1)}, bf16[2,4,2,64,256]{4,3,2,1,0:T(8,128)(2,1)S(1)}, u32[]{:S(2)}, u32[]{:S(2)}) collective-permute-start(bf16[2,4,2,64,256]{4,3,2,1,0:T(8,128)(2,1)S(1)} %get-tuple-element.12.refs_2_), channel_id=1, source_target_pairs={{0,96},{32,0},{64,32},{96,64},{1,97},{33,1},{65,33},{97,65},{2,98}... | collective-permute-start | bytes 1572872 | tf_op jit(solution)/shard_map/ppermute | solution.py:128
  105.2 18.6 %collective-permute-start.30 = (bf16[2,4,2,64,256]{4,3,2,1,0:T(8,128)(2,1)S(1)}, bf16[2,4,2,64,256]{4,3,2,1,0:T(8,128)(2,1)S(1)}, u32[]{:S(2)}, u32[]{:S(2)}) collective-permute-start(bf16[2,4,2,64,256]{4,3,2,1,0:T(8,128)(2,1)S(1)} %get-tuple-element.12.refs_2_), channel_id=1, source_target_pairs={{0,32},{32,64},{64,96},{96,0},{1,33},{33,65},{65,97},{97,1},{2,34}... | collective-permute-start | bytes 1572872 | tf_op jit(solution)/shard_map/ppermute | solution.py:128
  109.2 94.8 %collective-permute-start.10 = (bf16[4,512,512]{2,1,0:T(8,128)(2,1)S(1)}, bf16[4,512,512]{2,1,0:T(8,128)(2,1)}, u32[]{:S(2)}, u32[]{:S(2)}) collective-permute-start(bf16[4,512,512]{2,1,0:T(8,128)(2,1)S(1)} %shard_map.46.refs_0_), channel_id=1, source_target_pairs={{0,1},{1,0},{2,3},{3,2},{4,5},{5,4},{6,7},{7,6},{8,9},{9,8},{10,11... | collective-permute-start | bytes 6291464 | tf_op jit(solution)/shard_map/ppermute | solution.py:128
  113.6 18.0 %collective-permute-start.29 = (bf16[2,4,2,64,256]{4,3,2,1,0:T(8,128)(2,1)S(1)}, bf16[2,4,2,64,256]{4,3,2,1,0:T(8,128)(2,1)S(1)}, u32[]{:S(2)}, u32[]{:S(2)}) collective-permute-start(bf16[2,4,2,64,256]{4,3,2,1,0:T(8,128)(2,1)S(1)} %get-tuple-element.16.refs_2_), channel_id=1, source_target_pairs={{0,96},{32,0},{64,32},{96,64},{1,97},{33,1},{65,33},{97,65},{2,98}... | collective-permute-start | bytes 1572872 | tf_op jit(solution)/shard_map/ppermute | solution.py:128
  131.6 21.8 %collective-permute-start.28 = (bf16[2,4,2,64,256]{4,3,2,1,0:T(8,128)(2,1)S(1)}, bf16[2,4,2,64,256]{4,3,2,1,0:T(8,128)(2,1)S(1)}, u32[]{:S(2)}, u32[]{:S(2)}) collective-permute-start(bf16[2,4,2,64,256]{4,3,2,1,0:T(8,128)(2,1)S(1)} %get-tuple-element.16.refs_2_), channel_id=1, source_target_pairs={{0,32},{32,64},{64,96},{96,0},{1,33},{33,65},{65,97},{97,1},{2,34}... | collective-permute-start | bytes 1572872 | tf_op jit(solution)/shard_map/ppermute | solution.py:128
  134.5 19.7 %collective-permute-start.49 = (bf16[512,256]{1,0:T(8,128)(2,1)S(1)}, bf16[512,256]{1,0:T(8,128)(2,1)S(1)}, u32[]{:S(2)}, u32[]{:S(2)}) collective-permute-start(bf16[512,256]{1,0:T(8,128)(2,1)S(1)} %get-tuple-element.19), channel_id=1, source_target_pairs={{0,64},{32,96},{64,0},{96,32},{1,65},{33,97},{65,1},{97,33},{2,66}... | collective-permute-start | bytes 786440 | tf_op jit(solution)/shard_map/ppermute | solution.py:128
  140.0 16.6 %collective-permute-start.47 = (bf16[512,256]{1,0:T(8,128)(2,1)S(1)}, bf16[512,256]{1,0:T(8,128)(2,1)S(1)}, u32[]{:S(2)}, u32[]{:S(2)}) collective-permute-start(bf16[512,256]{1,0:T(8,128)(2,1)S(1)} %get-tuple-element.20), channel_id=1, source_target_pairs={{0,32},{32,64},{64,96},{96,0},{1,33},{33,65},{65,97},{97,1},{2,34}... | collective-permute-start | bytes 786440 | tf_op jit(solution)/shard_map/ppermute | solution.py:128
  140.0 21.5 %collective-permute-start.39 = (bf16[512,256]{1,0:T(8,128)(2,1)S(1)}, bf16[512,256]{1,0:T(8,128)(2,1)S(1)}, u32[]{:S(2)}, u32[]{:S(2)}) collective-permute-start(bf16[512,256]{1,0:T(8,128)(2,1)S(1)} %get-tuple-element.22), channel_id=1, source_target_pairs={{0,64},{32,96},{64,0},{96,32},{1,65},{33,97},{65,1},{97,33},{2,66}... | collective-permute-start | bytes 786440 | tf_op jit(solution)/shard_map/ppermute | solution.py:128
  157.3 20.0 %collective-permute-start.46 = (bf16[1,4,2,64,256]{4,3,2,1,0:T(8,128)(2,1)}, bf16[1,4,2,64,256]{4,3,2,1,0:T(8,128)(2,1)}, u32[]{:S(2)}, u32[]{:S(2)}) collective-permute-start(bf16[1,4,2,64,256]{4,3,2,1,0:T(8,128)(2,1)} %slice.47), channel_id=1, source_target_pairs={{0,96},{32,0},{64,32},{96,64},{1,97},{33,1},{65,33},{97,65},{2,98}... | collective-permute-start | bytes 786440 | tf_op jit(solution)/shard_map/ppermute | solution.py:128
  162.3 19.7 %collective-permute-start.45 = (bf16[1,4,2,64,256]{4,3,2,1,0:T(8,128)(2,1)}, bf16[1,4,2,64,256]{4,3,2,1,0:T(8,128)(2,1)}, u32[]{:S(2)}, u32[]{:S(2)}) collective-permute-start(bf16[1,4,2,64,256]{4,3,2,1,0:T(8,128)(2,1)} %slice.46), channel_id=1, source_target_pairs={{0,32},{32,64},{64,96},{96,0},{1,33},{33,65},{65,97},{97,1},{2,34}... | collective-permute-start | bytes 786440 | tf_op jit(solution)/shard_map/ppermute | solution.py:128
  165.4 24.4 %collective-permute-start.37 = (bf16[512,256]{1,0:T(8,128)(2,1)S(1)}, bf16[512,256]{1,0:T(8,128)(2,1)S(1)}, u32[]{:S(2)}, u32[]{:S(2)}) collective-permute-start(bf16[512,256]{1,0:T(8,128)(2,1)S(1)} %copy-done.51), channel_id=1, source_target_pairs={{0,32},{32,64},{64,96},{96,0},{1,33},{33,65},{65,97},{97,1},{2,34}... | collective-permute-start | bytes 786440 | tf_op jit(solution)/shard_map/ppermute | solution.py:128
  165.5 38.5 %collective-permute-start.43 = (bf16[512,640]{1,0:T(8,128)(2,1)S(1)}, bf16[512,640]{1,0:T(8,128)(2,1)S(1)}, u32[]{:S(2)}, u32[]{:S(2)}) collective-permute-start(bf16[512,640]{1,0:T(8,128)(2,1)S(1)} %get-tuple-element.27), channel_id=1, source_target_pairs={{0,64},{32,96},{64,0},{96,32},{1,65},{33,97},{65,1},{97,33},{2,66}... | collective-permute-start | bytes 1966088 | tf_op jit(solution)/shard_map/ppermute | solution.py:128
  177.3 63.7 %collective-permute-start.44 = (f32[2,512,384]{2,1,0:T(8,128)S(1)}, f32[2,512,384]{2,1,0:T(8,128)S(1)}, u32[]{:S(2)}, u32[]{:S(2)}) collective-permute-start(f32[2,512,384]{2,1,0:T(8,128)S(1)} %copy-done.18), channel_id=1, source_target_pairs={{0,16},{16,0},{1,17},{17,1},{2,18},{18,2},{3,19},{19,3},{4,20},{20... | collective-permute-start | bytes 4718600 | tf_op jit(solution)/shard_map/ppermute | solution.py:128
  190.6 43.5 %collective-permute-start.50 = (f32[2,512,256]{2,1,0:T(8,128)S(1)}, f32[2,512,256]{2,1,0:T(8,128)S(1)}, u32[]{:S(2)}, u32[]{:S(2)}) collective-permute-start(f32[2,512,256]{2,1,0:T(8,128)S(1)} %shard_map.51), channel_id=1, source_target_pairs={{0,16},{16,0},{1,17},{17,1},{2,18},{18,2},{3,19},{19,3},{4,20},{20... | collective-permute-start | bytes 3145736 | tf_op jit(solution)/shard_map/ppermute | solution.py:128
  201.1 44.9 %collective-permute-start.40 = (f32[2,512,256]{2,1,0:T(8,128)S(1)}, f32[2,512,256]{2,1,0:T(8,128)S(1)}, u32[]{:S(2)}, u32[]{:S(2)}) collective-permute-start(f32[2,512,256]{2,1,0:T(8,128)S(1)} %shard_map.49), channel_id=1, source_target_pairs={{0,16},{16,0},{1,17},{17,1},{2,18},{18,2},{3,19},{19,3},{4,20},{20... | collective-permute-start | bytes 3145736 | tf_op jit(solution)/shard_map/ppermute | solution.py:128
  204.1 17.0 %collective-permute-start.41 = (bf16[512,640]{1,0:T(8,128)(2,1)S(1)}, bf16[512,640]{1,0:T(8,128)(2,1)S(1)}, u32[]{:S(2)}, u32[]{:S(2)}) collective-permute-start(bf16[512,640]{1,0:T(8,128)(2,1)S(1)} %get-tuple-element.29), channel_id=1, source_target_pairs={{0,32},{32,64},{64,96},{96,0},{1,33},{33,65},{65,97},{97,1},{2,34}... | collective-permute-start | bytes 1966088 | tf_op jit(solution)/shard_map/ppermute | solution.py:128
  219.4 26.6 %collective-permute-start.36 = (bf16[512,256]{1,0:T(8,128)(2,1)S(1)}, bf16[512,256]{1,0:T(8,128)(2,1)S(1)}, u32[]{:S(2)}, u32[]{:S(2)}) collective-permute-start(bf16[512,256]{1,0:T(8,128)(2,1)S(1)} %get-tuple-element.31), channel_id=1, source_target_pairs={{0,64},{32,96},{64,0},{96,32},{1,65},{33,97},{65,1},{97,33},{2,66}... | collective-permute-start | bytes 786440 | tf_op jit(solution)/shard_map/ppermute | solution.py:128
  221.0 24.9 %collective-permute-start.35 = (bf16[512,256]{1,0:T(8,128)(2,1)S(1)}, bf16[512,256]{1,0:T(8,128)(2,1)S(1)}, u32[]{:S(2)}, u32[]{:S(2)}) collective-permute-start(bf16[512,256]{1,0:T(8,128)(2,1)S(1)} %get-tuple-element.32), channel_id=1, source_target_pairs={{0,96},{32,0},{64,32},{96,64},{1,97},{33,1},{65,33},{97,65},{2,98}... | collective-permute-start | bytes 786440 | tf_op jit(solution)/shard_map/ppermute | solution.py:128
  (73 other events, 842.9 us)

commit v2 on v1

--- a/solution.py
+++ b/solution.py
@@ -19,19 +19,6 @@
 
 
 VMEM_LIMIT = 24 * 1024 * 1024
-
-
-def transpose_kernel(at_ref, *refs):
-    blocks, out_ref, rows_ref = refs[:-2], refs[-2], refs[-1]
-    models, tokens = blocks[0].shape[:2]
-    for m in range(models):
-        for n in range(YL):
-            yl = lax.rem(at_ref[1] + n, YL)
-            for k, step in enumerate((0, 3, 1, 2)):
-                z = lax.rem(at_ref[0] + step, Z)
-                rows_ref[m, z * YL + yl] = blocks[n * Z + k][m]
-        turned = rows_ref[m].reshape(rows_ref.shape[1] * tokens, rows_ref.shape[3])
-        out_ref[m] = turned.T
 
 
 def in_vmem(kernel, here, arrays, out_shape, scratch=()):
@@ -46,14 +33,49 @@
     )(here, *arrays)
 
 
+def in_hbm(arrays):
+    return [pltpu.with_memory_space_constraint(a, pltpu.HBM) for a in arrays]
+
+
+def transpose_kernel(at_ref, *refs):
+    blocks, (out_ref, rows_ref, turned_ref, sems) = refs[:-4], refs[-4:]
+    copies = []
+    for n in range(YL):
+        yl = lax.rem(at_ref[1] + n, YL)
+        for k, step in enumerate((0, 3, 1, 2)):
+            z = lax.rem(at_ref[0] + step, Z)
+            b = n * Z + k
+            copies.append(pltpu.make_async_copy(blocks[b], rows_ref.at[:, z * YL + yl], sems.at[b]))
+            copies[-1].start()
+    for copy in copies:
+        copy.wait()
+    models, count, tokens, width = rows_ref.shape
+    outs = []
+    for m in range(models):
+        turned_ref[m] = rows_ref[m].reshape(count * tokens, width).T
+        outs.append(pltpu.make_async_copy(turned_ref.at[m], out_ref.at[m], sems.at[m]))
+        outs[-1].start()
+    for out in outs:
+        out.wait()
+
+
 def transposed(here, blocks):
     m, t, r = blocks[0].shape
     dtype = blocks[0].dtype
-    return in_vmem(
-        transpose_kernel, here, blocks,
-        jax.ShapeDtypeStruct((m, r, Z * YL * t), dtype),
-        [pltpu.VMEM((m, Z * YL, t, r), dtype)],
-    )
+    return pl.pallas_call(
+        transpose_kernel,
+        out_shape=jax.ShapeDtypeStruct((m, r, Z * YL * t), dtype),
+        in_specs=[pl.BlockSpec(memory_space=pltpu.SMEM)]
+        + [pl.BlockSpec(memory_space=pltpu.HBM) for _ in blocks],
+        out_specs=pl.BlockSpec(memory_space=pltpu.HBM),
+        scratch_shapes=[
+            pltpu.VMEM((m, Z * YL, t, r), dtype),
+            pltpu.VMEM((m, r, Z * YL * t), dtype),
+            pltpu.SemaphoreType.DMA((len(blocks),)),
+        ],
+        compiler_params=pltpu.CompilerParams(vmem_limit_bytes=VMEM_LIMIT),
+        name="transpose_acts",
+    )(here, *in_hbm(blocks))
 
 
 def sums(at_ref, a_refs, c_refs, w_refs, at, row, width):
@@ -178,8 +200,9 @@
         return own, send("x", X, 1, own), send("x", X, -1, own)
 
     def far(own, left, right):
-        far0 = send("x", X, 1, left[:1])
-        far1 = send("x", X, -1, right[1:])
+        near0, near1 = left[:1], right[1:]
+        far0 = send("x", X, 1, near0)
+        far1 = send("x", X, -1, near1)
         layout = [[(0, 0), (0, 1)], [(1, 0), (1, 1)], [(2, 0), (2, 1)], [(3, 0), (4, 0)]]
         return layout, [own, left, right, far0, far1]
 
@@ -208,24 +231,20 @@
     c0 = columns_for(*first)
     c12 = columns_for(*rest)
     grads = [split(c0)]
-    nears = []
+    partials = [partial(0, grads[0])]
+    c12 = after(partials[0], c12)
+    late = after(partials[0], weights[0])
     for n, (start, width) in enumerate(CHUNKS[1:], 1):
         at = start - rest[0]
-        nears.append(near(c12[..., at:at + width]))
-
-    partials = [partial(0, grads[0])]
-    nears = after(partials[0], nears)
-    late = after(partials[0], weights[0])
-    grads += [far(*nears[n - 1]) for n in (1, 2)]
-    last = CHUNKS[-1]
-    wo = [weights_for(y, 0, last[0], late), weights_for(y, *last, late)]
+        part = c12[..., at:at + width]
+        grads.append(split(part) if n == 1 else far(*near(part)))
+    wo = [weights_for(y, *chunk, late) for chunk in CHUNKS]
     partials += [partial(n, grads[n]) for n in (1, 2)]
     sent = [send("yh", YH, 1, p) for p in partials]
     outs = []
     for n, (start, width) in enumerate(CHUNKS):
-        final = n == len(CHUNKS) - 1
-        w, at = (wo[1], 0) if final else (wo[0], start)
-        outs.append(merge(here, a_own, grads[n], w, at, sent[n], outs if final else []))
+        earlier = outs if n == len(CHUNKS) - 1 else []
+        outs.append(merge(here, a_own, grads[n], wo[n], 0, sent[n], earlier))
     return outs[-1]
 
 

time: 253 us -> 257 us (1.016)
  starting transfers between devices: 73.6 us -> 96.7 us
  waiting for transfers between devices: 111 us -> 97.9 us
  local copies, waits for them, and re-layouts: 33.5 us -> 24.9 us
  Pallas kernels: 28.8 us -> 33.2 us
    ppermute x51 -> x56, starting transfers between devices: 62.8 us -> 88.5 us  [send(): lax.ppermute(value, axis, [(i, (i + step) % size) for i in range(size)])]
    ppermute x51 -> x56, waiting for transfers between devices: 111 us -> 97.9 us  [send(): lax.ppermute(value, axis, [(i, (i + step) % size) for i in range(size)])]
    pallas_call x0 -> x2, Pallas kernels: none -> 6.64 us  [transposed(): pl.pallas_call(transpose_kernel, out_shape=jax.ShapeDtypeStruct((m, r, Z...]
    unnamed x107 -> x95, local copies, waits for them, and re-layouts: 17.7 us -> 11.2 us
    all_to_all x2, starting transfers between devices: 10.8 us -> 8.19 us  [columns_for(): moved = lax.all_to_all(cut, fsdp, split_axis=1, concat_axis=0, tiled=True)]
    pallas_call x8 -> x6, Pallas kernels: 28.8 us -> 26.6 us  [in_vmem(): pl.pallas_call(kernel, out_shape=out_shape, in_specs=[pl.BlockSpec(memory...]
  transfers between devices with their start and end apart: 53 -> 58, of which waited for: 24 -> 22; matrix products, arithmetic and copies ran while one was open for 9% -> 7% of each run, Pallas kernels for 10% -> 10%
where the time goes in v2:
time: 257 us; the launch traced here: 256 us
  waiting for transfers between devices  97.9 us (38%)
  starting transfers between devices  96.7 us (38%)
  Pallas kernels  33.2 us (13%)
  local copies, waits for them, and re-layouts  24.9 us (10%)
  other arithmetic  2.96 us (1%)
    ppermute x56, waiting for transfers between devices, send(): lax.ppermute(value, axis, [(i, (i + step) % size) for i in range(size)])  97.9 us
    ppermute x56, starting transfers between devices, send(): lax.ppermute(value, axis, [(i, (i + step) % size) for i in range(size)])  88.5 us
    pallas_call x6, Pallas kernels, in_vmem(): pl.pallas_call(kernel, out_shape=out_shape, in_specs=[pl.BlockSpec(memory...  26.6 us
    unnamed x95, local copies, waits for them, and re-layouts  11.2 us
    dynamic_slice x4, local copies, waits for them, and re-layouts, piece(): return lax.dynamic_slice(source, (base, start), (rows, width))  8.34 us
    all_to_all x2, starting transfers between devices, columns_for(): moved = lax.all_to_all(cut, fsdp, split_axis=1, concat_axis=0, tiled=True)  8.19 us
    pallas_call x2, Pallas kernels, transposed(): pl.pallas_call(transpose_kernel, out_shape=jax.ShapeDtypeStruct((m, r, Z...  6.64 us
  transfers between devices with their start and end apart: 58, of which 22 were waited for; matrix products, arithmetic and copies ran while one was open for 7% of the time, Pallas kernels for 10%

profile of v2, /device:TPU:0, one launch (start us, length us, event | category | flops | bytes accessed | tf_op | source)
XLA Modules:
  0.0 256.3 jit_solution(13786834751340024024)
XLA Ops:
  9.4 2.8 %collective-permute-done.2 = bf16[64,1024]{1,0:T(8,128)(2,1)S(1)} collective-permute-done((bf16[64,1024]{1,0:T(8,128)(2,1)S(1)}, bf16[64,1024]{1,0:T(8,128)(2,1)S(1)}, u32[]{:S(2)}, u32[]{:S(2)}) %collective-permute-start.2) | collective-permute-done | bytes 131104 | tf_op jit(solution)/shard_map/ppermute | solution.py:150
  25.5 6.4 %collective-permute-start.17 = (bf16[4,64,512]{2,1,0:T(8,128)(2,1)S(1)}, bf16[4,64,512]{2,1,0:T(8,128)(2,1)S(1)}, u32[]{:S(2)}, u32[]{:S(2)}) collective-permute-start(bf16[4,64,512]{2,1,0:T(8,128)(2,1)S(1)} %collective-permute-done.14.refs_4_), channel_id=1, source_target_pairs={{0,8},{4,12},{8,0},{12,4},{1,9},{5,13},{9,1},{13,5},{2,10},{6,14},... | collective-permute-start | bytes 786440 | tf_op jit(solution)/shard_map/ppermute | solution.py:150
  32.4 3.2 %collective-permute-done.15.refs_5_ = bf16[4,64,512]{2,1,0:T(8,128)(2,1)S(1)} collective-permute-done((bf16[4,64,512]{2,1,0:T(8,128)(2,1)S(1)}, bf16[4,64,512]{2,1,0:T(8,128)(2,1)S(1)}, u32[]{:S(2)}, u32[]{:S(2)}) %collective-permute-start.15) | collective-permute-done | bytes 262176 | tf_op jit(solution)/shard_map/ppermute | solution.py:150
  35.5 4.1 %collective-permute-done.16.refs_6_ = bf16[4,64,512]{2,1,0:T(8,128)(2,1)S(1)} collective-permute-done((bf16[4,64,512]{2,1,0:T(8,128)(2,1)S(1)}, bf16[4,64,512]{2,1,0:T(8,128)(2,1)S(1)}, u32[]{:S(2)}, u32[]{:S(2)}) %collective-permute-start.16) | collective-permute-done | bytes 262176 | tf_op jit(solution)/shard_map/ppermute | solution.py:150
  42.4 3.6 %transpose_acts.3.refs_0_ = bf16[4,512,512]{2,1,0:T(8,128)(2,1)} custom-call(s32[3]{0:T(128)S(1)} %pad_add_fusion.at_ref, bf16[4,64,512]{2,1,0:T(8,128)(2,1)} %copy-done.33, bf16[4,64,512]{2,1,0:T(8,128)(2,1)} %copy-done.39, bf16[4,64,512]{2,1,0:T(8,128)(2,1)} %copy-done.40, bf16[4,64,512]{2,1,0:T(8,128)(2,1)} %copy-done.42, bf16[4,64,512]{2,1,0:T(8,128)(2,1)} %copy-done.38, ...), custom_call_target="tpu_custom_call" | custom-call | tf_op jit(solution)/shard_map/transpose_acts/pallas_call | solution.py:65
  47.5 3.9 %all-to-all-start = ((bf16[64,16,384]{2,0,1:T(8,128)(2,1)}), bf16[64,16,384]{2,0,1:T(8,128)(2,1)S(1)}, u32[]{:S(2)}, u32[]{:S(2)}) async-start(bf16[64,16,384]{2,0,1:T(8,128)(2,1)} %copy.7), calls=%async_computation | async-start | bytes 1572864 | tf_op jit(solution)/shard_map/all_to_all | solution.py:196
  57.4 2.9 %collective-permute-start.26 = (bf16[512,384]{1,0:T(8,128)(2,1)S(1)}, bf16[512,384]{1,0:T(8,128)(2,1)S(1)}, u32[]{:S(2)}, u32[]{:S(2)}) collective-permute-start(bf16[512,384]{1,0:T(8,128)(2,1)S(1)} %get-tuple-element.30), channel_id=1, source_target_pairs={{0,96},{32,0},{64,32},{96,64},{1,97},{33,1},{65,33},{97,65},{2,98}... | collective-permute-start | bytes 1179656 | tf_op jit(solution)/shard_map/ppermute | solution.py:150
  60.3 8.2 %collective-permute-done.6.refs_4_ = bf16[4,64,512]{2,1,0:T(8,128)(2,1)S(1)} collective-permute-done((bf16[4,64,512]{2,1,0:T(8,128)(2,1)S(1)}, bf16[4,64,512]{2,1,0:T(8,128)(2,1)S(1)}, u32[]{:S(2)}, u32[]{:S(2)}) %collective-permute-start.6) | collective-permute-done | bytes 262176 | tf_op jit(solution)/shard_map/ppermute | solution.py:150
  72.2 10.0 %collective-permute-done.4.refs_2_ = bf16[4,64,512]{2,1,0:T(8,128)(2,1)S(1)} collective-permute-done((bf16[4,64,512]{2,1,0:T(8,128)(2,1)S(1)}, bf16[4,64,512]{2,1,0:T(8,128)(2,1)S(1)}, u32[]{:S(2)}, u32[]{:S(2)}) %collective-permute-start.4) | collective-permute-done | bytes 262176 | tf_op jit(solution)/shard_map/ppermute | solution.py:150
  90.8 4.3 %all-to-all-start.1 = ((bf16[64,16,512]{2,0,1:T(8,128)(2,1)}), bf16[64,16,512]{2,0,1:T(8,128)(2,1)}, u32[]{:S(2)}, u32[]{:S(2)}) async-start(bf16[64,16,512]{2,0,1:T(8,128)(2,1)} %copy.8), calls=%async_computation.1 | async-start | bytes 2097152 | tf_op jit(solution)/shard_map/all_to_all | solution.py:196
  99.7 3.0 %transpose_acts.2.refs_0_ = bf16[4,512,512]{2,1,0:T(8,128)(2,1)S(1)} custom-call(s32[3]{0:T(128)S(1)} %pad_add_fusion.at_ref, bf16[4,64,512]{2,1,0:T(8,128)(2,1)} %copy-done.32, bf16[4,64,512]{2,1,0:T(8,128)(2,1)} %copy-done.35, bf16[4,64,512]{2,1,0:T(8,128)(2,1)} %copy-done.36, bf16[4,64,512]{2,1,0:T(8,128)(2,1)} %copy-done.37, ...), custom_call_target="tpu_custom_call" | custom-call | tf_op jit(solution)/shard_map/transpose_acts/pallas_call | solution.py:65
  103.0 5.5 %collective-permute-done.19.refs_3_ = bf16[1,4,2,64,384]{4,3,2,1,0:T(8,128)(2,1)S(1)} collective-permute-done((bf16[1,4,2,64,384]{4,3,2,1,0:T(8,128)(2,1)S(1)}, bf16[1,4,2,64,384]{4,3,2,1,0:T(8,128)(2,1)S(1)}, u32[]{:S(2)}, u32[]{:S(2)}) %collective-permute-start.19) | collective-permute-done | bytes 393248 | tf_op jit(solution)/shard_map/ppermute | solution.py:150
  110.6 6.4 %collective-permute-done.20.refs_4_ = bf16[1,4,2,64,384]{4,3,2,1,0:T(8,128)(2,1)S(1)} collective-permute-done((bf16[1,4,2,64,384]{4,3,2,1,0:T(8,128)(2,1)S(1)}, bf16[1,4,2,64,384]{4,3,2,1,0:T(8,128)(2,1)S(1)}, u32[]{:S(2)}, u32[]{:S(2)}) %collective-permute-start.20) | collective-permute-done | bytes 393248 | tf_op jit(solution)/shard_map/ppermute | solution.py:150
  118.6 2.9 %dynamic-slice_bitcast_fusion.4 = (bf16[512,256]{1,0:T(8,128)(2,1)}, bf16[512,256]{1,0:T(8,128)(2,1)}, bf16[512,256]{1,0:T(8,128)(2,1)}, bf16[512,256]{1,0:T(8,1...) fusion(bf16[1,4096,896]{2,1,0:T(8,128)(2,1)} %param.4, ...), kind=kLoop, calls=%fused_computation.5 | loop fusion | bytes 4194320 | tf_op jit(solution)/shard_map/dynamic_slice | solution.py:190
  121.9 3.5 %collective-permute-done.23.refs_7_ = bf16[1,4,2,64,384]{4,3,2,1,0:T(8,128)(2,1)S(1)} collective-permute-done((bf16[1,4,2,64,384]{4,3,2,1,0:T(8,128)(2,1)S(1)}, bf16[1,4,2,64,384]{4,3,2,1,0:T(8,128)(2,1)S(1)}, u32[]{:S(2)}, u32[]{:S(2)}) %collective-permute-start.23) | collective-permute-done | bytes 393248 | tf_op jit(solution)/shard_map/ppermute | solution.py:150
  130.4 6.3 %shard_map.46 = f32[2,512,384]{2,1,0:T(8,128)} custom-call(s32[3]{0:T(128)S(1)} %pad_add_fusion.at_ref, bf16[4,512,512]{2,1,0:T(8,128)(2,1)} %transpose_acts.3.refs_0_, bf16[4,512,512]{2,1,0:T(8,128)(2,1)} %collective-permute-done.18.refs_1_, bf16[2,4,2,64,384]{4,3,2,1,0:T(8,128)(2,1)S(1)} %bitcast.55, ...), custom_call_target="tpu_custom_call" | custom-call | tf_op jit(solution)/shard_map/pallas_call | solution.py:25
  142.8 2.9 %collective-permute-start.46 = (bf16[1,4,2,64,256]{4,3,2,1,0:T(8,128)(2,1)S(1)}, bf16[1,4,2,64,256]{4,3,2,1,0:T(8,128)(2,1)}, u32[]{:S(2)}, u32[]{:S(2)}) collective-permute-start(bf16[1,4,2,64,256]{4,3,2,1,0:T(8,128)(2,1)S(1)} %get-tuple-element.33), channel_id=1, source_target_pairs={{0,96},{32,0},{64,32},{96,64},{1,97},{33,1},{65,33},{97,65},{2,98}... | collective-permute-start | bytes 786440 | tf_op jit(solution)/shard_map/ppermute | solution.py:150
  158.6 8.3 %collective-permute-done.44.refs_4_ = bf16[1,4,2,64,256]{4,3,2,1,0:T(8,128)(2,1)S(1)} collective-permute-done((bf16[1,4,2,64,256]{4,3,2,1,0:T(8,128)(2,1)S(1)}, bf16[1,4,2,64,256]{4,3,2,1,0:T(8,128)(2,1)S(1)}, u32[]{:S(2)}, u32[]{:S(2)}) %collective-permute-start.44) | collective-permute-done | bytes 262176 | tf_op jit(solution)/shard_map/ppermute | solution.py:150
  169.8 3.0 %collective-permute-start.48 = (bf16[1,4,2,64,256]{4,3,2,1,0:T(8,128)(2,1)}, bf16[1,4,2,64,256]{4,3,2,1,0:T(8,128)(2,1)}, u32[]{:S(2)}, u32[]{:S(2)}) collective-permute-start(bf16[1,4,2,64,256]{4,3,2,1,0:T(8,128)(2,1)} %collective-permute-done.46.refs_6_), channel_id=1, source_target_pairs={{0,96},{32,0},{64,32},{96,64},{1,97},{33,1},{65,33},{97,65},{2,98}... | collective-permute-start | bytes 786440 | tf_op jit(solution)/shard_map/ppermute | solution.py:150
  172.8 3.1 %collective-permute-start.42 = (f32[2,512,384]{2,1,0:T(8,128)}, f32[2,512,384]{2,1,0:T(8,128)}, u32[]{:S(2)}, u32[]{:S(2)}) collective-permute-start(f32[2,512,384]{2,1,0:T(8,128)} %shard_map.46), channel_id=1, source_target_pairs={{0,16},{16,0},{1,17},{17,1},{2,18},{18,2},{3,19},{19,3},{4,20},{20... | collective-permute-start | bytes 4718600 | tf_op jit(solution)/shard_map/ppermute | solution.py:150
  179.7 3.6 %collective-permute-done.48.refs_8_ = bf16[1,4,2,64,256]{4,3,2,1,0:T(8,128)(2,1)} collective-permute-done((bf16[1,4,2,64,256]{4,3,2,1,0:T(8,128)(2,1)}, bf16[1,4,2,64,256]{4,3,2,1,0:T(8,128)(2,1)}, u32[]{:S(2)}, u32[]{:S(2)}) %collective-permute-start.48) | collective-permute-done | bytes 262176 | tf_op jit(solution)/shard_map/ppermute | solution.py:150
  183.3 4.3 %collective-permute-start.31 = (bf16[1,4,2,64,256]{4,3,2,1,0:T(8,128)(2,1)S(1)}, bf16[1,4,2,64,256]{4,3,2,1,0:T(8,128)(2,1)S(1)}, u32[]{:S(2)}, u32[]{:S(2)}) collective-permute-start(bf16[1,4,2,64,256]{4,3,2,1,0:T(8,128)(2,1)S(1)} %slice.55), channel_id=1, source_target_pairs={{0,96},{32,0},{64,32},{96,64},{1,97},{33,1},{65,33},{97,65},{2,98}... | collective-permute-start | bytes 786440 | tf_op jit(solution)/shard_map/ppermute | solution.py:150
  189.3 4.0 %shard_map.49 = f32[2,512,256]{2,1,0:T(8,128)S(1)} custom-call(s32[3]{0:T(128)S(1)} %pad_add_fusion.at_ref, bf16[4,512,512]{2,1,0:T(8,128)(2,1)} %transpose_acts.3.refs_0_, bf16[4,512,512]{2,1,0:T(8,128)(2,1)} %collective-permute-done.18.refs_1_, bf16[2,4,2,64,256]{4,3,2,1,0:T(8,128)(2,1)S(1)} %copy-done, ...), custom_call_target="tpu_custom_call" | custom-call | tf_op jit(solution)/shard_map/pallas_call | solution.py:25
  193.8 3.2 %collective-permute-start.50 = (bf16[512,256]{1,0:T(8,128)(2,1)S(1)}, bf16[512,256]{1,0:T(8,128)(2,1)S(1)}, u32[]{:S(2)}, u32[]{:S(2)}) collective-permute-start(bf16[512,256]{1,0:T(8,128)(2,1)S(1)} %get-tuple-element.18), channel_id=1, source_target_pairs={{0,96},{32,0},{64,32},{96,64},{1,97},{33,1},{65,33},{97,65},{2,98}... | collective-permute-start | bytes 786440 | tf_op jit(solution)/shard_map/ppermute | solution.py:150
  198.7 3.7 %shard_map.47 = f32[2,512,256]{2,1,0:T(8,128)S(1)} custom-call(s32[3]{0:T(128)S(1)} %pad_add_fusion.at_ref, bf16[4,512,512]{2,1,0:T(8,128)(2,1)} %transpose_acts.3.refs_0_, bf16[4,512,512]{2,1,0:T(8,128)(2,1)} %collective-permute-done.18.refs_1_, bf16[2,4,2,64,256]{4,3,2,1,0:T(8,128)(2,1)S(1)} %get-tuple-element.36.refs_2_, ...), custom_call_target="tpu_custom_call" | custom-call | tf_op jit(solution)/shard_map/pallas_call | solution.py:25
  207.6 9.7 %collective-permute-done.51.refs_12_ = bf16[512,256]{1,0:T(8,128)(2,1)S(1)} collective-permute-done((bf16[512,256]{1,0:T(8,128)(2,1)S(1)}, bf16[512,256]{1,0:T(8,128)(2,1)S(1)}, u32[]{:S(2)}, u32[]{:S(2)}) %collective-permute-start.51) | collective-permute-done | bytes 262176 | tf_op jit(solution)/shard_map/ppermute | solution.py:150
  219.8 15.2 %collective-permute-done.40.refs_11_ = bf16[512,384]{1,0:T(8,128)(2,1)S(1)} collective-permute-done((bf16[512,384]{1,0:T(8,128)(2,1)S(1)}, bf16[512,384]{1,0:T(8,128)(2,1)S(1)}, u32[]{:S(2)}, u32[]{:S(2)}) %collective-permute-start.40) | collective-permute-done | bytes 393248 | tf_op jit(solution)/shard_map/ppermute | solution.py:150
  234.9 3.7 %collective-permute-start.33 = (bf16[512,256]{1,0:T(8,128)(2,1)S(1)}, bf16[512,256]{1,0:T(8,128)(2,1)S(1)}, u32[]{:S(2)}, u32[]{:S(2)}) collective-permute-start(bf16[512,256]{1,0:T(8,128)(2,1)S(1)} %get-tuple-element.22), channel_id=1, source_target_pairs={{0,96},{32,0},{64,32},{96,64},{1,97},{33,1},{65,33},{97,65},{2,98}... | collective-permute-start | bytes 786440 | tf_op jit(solution)/shard_map/ppermute | solution.py:150
  240.2 3.5 %shard_map.50.refs_13_ = bf16[512,256]{1,0:T(8,128)(2,1)S(1)} custom-call(s32[3]{0:T(128)S(1)} %pad_add_fusion.at_ref, bf16[4,512,512]{2,1,0:T(8,128)(2,1)S(1)} %transpose_acts.2.refs_0_, bf16[4,512,512]{2,1,0:T(8,128)(2,1)} %collective-permute-done.10.refs_1_, bf16[2,4,2,64,256]{4,3,2,1,0:T(8,128)(2,1)S(1)} %copy-done, ...), custom_call_target="tpu_custom_call" | custom-call | tf_op jit(solution)/shard_map/pallas_call | solution.py:25
  243.8 5.0 %shard_map.48.refs_12_ = bf16[512,384]{1,0:T(8,128)(2,1)S(1)} custom-call(s32[3]{0:T(128)S(1)} %pad_add_fusion.at_ref, bf16[4,512,512]{2,1,0:T(8,128)(2,1)S(1)} %transpose_acts.2.refs_0_, bf16[4,512,512]{2,1,0:T(8,128)(2,1)} %collective-permute-done.10.refs_1_, bf16[2,4,2,64,384]{4,3,2,1,0:T(8,128)(2,1)S(1)} %bitcast.56, ...), custom_call_target="tpu_custom_call" | custom-call | tf_op jit(solution)/shard_map/pallas_call | solution.py:25
  248.8 3.5 %collective-permute-done.38.refs_11_ = f32[2,512,256]{2,1,0:T(8,128)S(1)} collective-permute-done((f32[2,512,256]{2,1,0:T(8,128)S(1)}, f32[2,512,256]{2,1,0:T(8,128)S(1)}, u32[]{:S(2)}, u32[]{:S(2)}) %collective-permute-start.38) | collective-permute-done | bytes 1048608 | tf_op jit(solution)/shard_map/ppermute | solution.py:150
  252.3 4.1 %shard_map.51 = bf16[512,896]{1,0:T(8,128)(2,1)} custom-call(s32[3]{0:T(128)S(1)} %pad_add_fusion.at_ref, bf16[4,512,512]{2,1,0:T(8,128)(2,1)S(1)} %transpose_acts.2.refs_0_, bf16[4,512,512]{2,1,0:T(8,128)(2,1)} %collective-permute-done.10.refs_1_, bf16[2,4,2,64,256]{4,3,2,1,0:T(8,128)(2,1)S(1)} %get-tuple-element.36.refs_2_, ...), custom_call_target="tpu_custom_call" | custom-call | tf_op jit(solution)/shard_map/pallas_call | solution.py:25
  (204 shorter events, 97.8 us)
Async XLA Ops:
  16.0 16.0 %collective-permute-start.12 = (bf16[4,64,512]{2,1,0:T(8,128)(2,1)S(1)}, bf16[4,64,512]{2,1,0:T(8,128)(2,1)S(1)}, u32[]{:S(2)}, u32[]{:S(2)}) collective-permute-start(bf16[4,64,512]{2,1,0:T(8,128)(2,1)S(1)} %get-tuple-element.42.refs_0_), channel_id=1, source_target_pairs={{0,12},{4,0},{8,4},{12,8},{1,13},{5,1},{9,5},{13,9},{2,14},{6,2},{... | collective-permute-start | bytes 786440 | tf_op jit(solution)/shard_map/ppermute | solution.py:150
  18.1 14.3 %collective-permute-start.13 = (bf16[4,64,512]{2,1,0:T(8,128)(2,1)S(1)}, bf16[4,64,512]{2,1,0:T(8,128)(2,1)S(1)}, u32[]{:S(2)}, u32[]{:S(2)}) collective-permute-start(bf16[4,64,512]{2,1,0:T(8,128)(2,1)S(1)} %get-tuple-element.42.refs_0_), channel_id=1, source_target_pairs={{0,8},{4,12},{8,0},{12,4},{1,9},{5,13},{9,1},{13,5},{2,10},{6,14},... | collective-permute-start | bytes 786440 | tf_op jit(solution)/shard_map/ppermute | solution.py:150
  20.0 15.6 %collective-permute-start.15 = (bf16[4,64,512]{2,1,0:T(8,128)(2,1)S(1)}, bf16[4,64,512]{2,1,0:T(8,128)(2,1)S(1)}, u32[]{:S(2)}, u32[]{:S(2)}) collective-permute-start(bf16[4,64,512]{2,1,0:T(8,128)(2,1)S(1)} %collective-permute-done.14.refs_4_), channel_id=1, source_target_pairs={{0,4},{4,8},{8,12},{12,0},{1,5},{5,9},{9,13},{13,1},{2,6},{6,10},{... | collective-permute-start | bytes 786440 | tf_op jit(solution)/shard_map/ppermute | solution.py:150
  21.9 17.8 %collective-permute-start.16 = (bf16[4,64,512]{2,1,0:T(8,128)(2,1)S(1)}, bf16[4,64,512]{2,1,0:T(8,128)(2,1)S(1)}, u32[]{:S(2)}, u32[]{:S(2)}) collective-permute-start(bf16[4,64,512]{2,1,0:T(8,128)(2,1)S(1)} %collective-permute-done.14.refs_4_), channel_id=1, source_target_pairs={{0,12},{4,0},{8,4},{12,8},{1,13},{5,1},{9,5},{13,9},{2,14},{6,2},{... | collective-permute-start | bytes 786440 | tf_op jit(solution)/shard_map/ppermute | solution.py:150
  25.5 16.1 %collective-permute-start.17 = (bf16[4,64,512]{2,1,0:T(8,128)(2,1)S(1)}, bf16[4,64,512]{2,1,0:T(8,128)(2,1)S(1)}, u32[]{:S(2)}, u32[]{:S(2)}) collective-permute-start(bf16[4,64,512]{2,1,0:T(8,128)(2,1)S(1)} %collective-permute-done.14.refs_4_), channel_id=1, source_target_pairs={{0,8},{4,12},{8,0},{12,4},{1,9},{5,13},{9,1},{13,5},{2,10},{6,14},... | collective-permute-start | bytes 786440 | tf_op jit(solution)/shard_map/ppermute | solution.py:150
  46.0 82.9 %collective-permute-start.18 = (bf16[4,512,512]{2,1,0:T(8,128)(2,1)}, bf16[4,512,512]{2,1,0:T(8,128)(2,1)}, u32[]{:S(2)}, u32[]{:S(2)}) collective-permute-start(bf16[4,512,512]{2,1,0:T(8,128)(2,1)} %transpose_acts.3.refs_0_), channel_id=1, source_target_pairs={{0,1},{1,0},{2,3},{3,2},{4,5},{5,4},{6,7},{7,6},{8,9},{9,8},{10,11... | collective-permute-start | bytes 6291464 | tf_op jit(solution)/shard_map/ppermute | solution.py:150
  47.5 43.3 %all-to-all-start = ((bf16[64,16,384]{2,0,1:T(8,128)(2,1)}), bf16[64,16,384]{2,0,1:T(8,128)(2,1)S(1)}, u32[]{:S(2)}, u32[]{:S(2)}) async-start(bf16[64,16,384]{2,0,1:T(8,128)(2,1)} %copy.7), calls=%async_computation | async-start | bytes 1572864 | tf_op jit(solution)/shard_map/all_to_all | solution.py:196
  51.4 17.2 %collective-permute-start.6 = (bf16[4,64,512]{2,1,0:T(8,128)(2,1)S(1)}, bf16[4,64,512]{2,1,0:T(8,128)(2,1)S(1)}, u32[]{:S(2)}, u32[]{:S(2)}) collective-permute-start(bf16[4,64,512]{2,1,0:T(8,128)(2,1)S(1)} %get-tuple-element.43.refs_0_), channel_id=1, source_target_pairs={{0,2},{2,0},{1,3},{3,1},{4,6},{6,4},{5,7},{7,5},{8,10},{10,8},{9,1... | collective-permute-start | bytes 786440 | tf_op jit(solution)/shard_map/ppermute | solution.py:150
  53.3 18.0 %collective-permute-start.3 = (bf16[4,64,512]{2,1,0:T(8,128)(2,1)S(1)}, bf16[4,64,512]{2,1,0:T(8,128)(2,1)S(1)}, u32[]{:S(2)}, u32[]{:S(2)}) collective-permute-start(bf16[4,64,512]{2,1,0:T(8,128)(2,1)S(1)} %get-tuple-element.43.refs_0_), channel_id=1, source_target_pairs={{0,4},{4,8},{8,12},{12,0},{1,5},{5,9},{9,13},{13,1},{2,6},{6,10},{... | collective-permute-start | bytes 786440 | tf_op jit(solution)/shard_map/ppermute | solution.py:150
  57.1 27.2 %collective-permute-start.25 = (bf16[512,384]{1,0:T(8,128)(2,1)S(1)}, bf16[512,384]{1,0:T(8,128)(2,1)S(1)}, u32[]{:S(2)}, u32[]{:S(2)}) collective-permute-start(bf16[512,384]{1,0:T(8,128)(2,1)S(1)} %get-tuple-element.31), channel_id=1, source_target_pairs={{0,32},{32,64},{64,96},{96,0},{1,33},{33,65},{65,97},{97,1},{2,34}... | collective-permute-start | bytes 1179656 | tf_op jit(solution)/shard_map/ppermute | solution.py:150
  57.4 29.6 %collective-permute-start.26 = (bf16[512,384]{1,0:T(8,128)(2,1)S(1)}, bf16[512,384]{1,0:T(8,128)(2,1)S(1)}, u32[]{:S(2)}, u32[]{:S(2)}) collective-permute-start(bf16[512,384]{1,0:T(8,128)(2,1)S(1)} %get-tuple-element.30), channel_id=1, source_target_pairs={{0,96},{32,0},{64,32},{96,64},{1,97},{33,1},{65,33},{97,65},{2,98}... | collective-permute-start | bytes 1179656 | tf_op jit(solution)/shard_map/ppermute | solution.py:150
  82.2 20.5 %collective-permute-start.27 = (bf16[512,384]{1,0:T(8,128)(2,1)}, bf16[512,384]{1,0:T(8,128)(2,1)}, u32[]{:S(2)}, u32[]{:S(2)}) collective-permute-start(bf16[512,384]{1,0:T(8,128)(2,1)} %get-tuple-element.29), channel_id=1, source_target_pairs={{0,64},{32,96},{64,0},{96,32},{1,65},{33,97},{65,1},{97,33},{2,66}... | collective-permute-start | bytes 1179656 | tf_op jit(solution)/shard_map/ppermute | solution.py:150
  90.8 48.2 %all-to-all-start.1 = ((bf16[64,16,512]{2,0,1:T(8,128)(2,1)}), bf16[64,16,512]{2,0,1:T(8,128)(2,1)}, u32[]{:S(2)}, u32[]{:S(2)}) async-start(bf16[64,16,512]{2,0,1:T(8,128)(2,1)} %copy.8), calls=%async_computation.1 | async-start | bytes 2097152 | tf_op jit(solution)/shard_map/all_to_all | solution.py:196
  98.8 18.2 %collective-permute-start.20 = (bf16[1,4,2,64,384]{4,3,2,1,0:T(8,128)(2,1)S(1)}, bf16[1,4,2,64,384]{4,3,2,1,0:T(8,128)(2,1)S(1)}, u32[]{:S(2)}, u32[]{:S(2)}) collective-permute-start(bf16[1,4,2,64,384]{4,3,2,1,0:T(8,128)(2,1)S(1)} %bitcast.65), channel_id=1, source_target_pairs={{0,32},{32,64},{64,96},{96,0},{1,33},{33,65},{65,97},{97,1},{2,34}... | collective-permute-start | bytes 1179656 | tf_op jit(solution)/shard_map/ppermute | solution.py:150
  102.8 90.9 %collective-permute-start.10 = (bf16[4,512,512]{2,1,0:T(8,128)(2,1)S(1)}, bf16[4,512,512]{2,1,0:T(8,128)(2,1)}, u32[]{:S(2)}, u32[]{:S(2)}) collective-permute-start(bf16[4,512,512]{2,1,0:T(8,128)(2,1)S(1)} %transpose_acts.2.refs_0_), channel_id=1, source_target_pairs={{0,1},{1,0},{2,3},{3,2},{4,5},{5,4},{6,7},{7,6},{8,9},{9,8},{10,11... | collective-permute-start | bytes 6291464 | tf_op jit(solution)/shard_map/ppermute | solution.py:150
  110.2 15.2 %collective-permute-start.23 = (bf16[1,4,2,64,384]{4,3,2,1,0:T(8,128)(2,1)S(1)}, bf16[1,4,2,64,384]{4,3,2,1,0:T(8,128)(2,1)S(1)}, u32[]{:S(2)}, u32[]{:S(2)}) collective-permute-start(bf16[1,4,2,64,384]{4,3,2,1,0:T(8,128)(2,1)S(1)} %collective-permute-done.19.refs_3_), channel_id=1, source_target_pairs={{0,32},{32,64},{64,96},{96,0},{1,33},{33,65},{65,97},{97,1},{2,34}... | collective-permute-start | bytes 1179656 | tf_op jit(solution)/shard_map/ppermute | solution.py:150
  121.4 18.7 %collective-permute-start.52 = (bf16[512,256]{1,0:T(8,128)(2,1)}, bf16[512,256]{1,0:T(8,128)(2,1)S(1)}, u32[]{:S(2)}, u32[]{:S(2)}) collective-permute-start(bf16[512,256]{1,0:T(8,128)(2,1)} %get-tuple-element.10), channel_id=1, source_target_pairs={{0,32},{32,64},{64,96},{96,0},{1,33},{33,65},{65,97},{97,1},{2,34}... | collective-permute-start | bytes 786440 | tf_op jit(solution)/shard_map/ppermute | solution.py:150
  125.4 17.1 %collective-permute-start.53 = (bf16[512,256]{1,0:T(8,128)(2,1)}, bf16[512,256]{1,0:T(8,128)(2,1)}, u32[]{:S(2)}, u32[]{:S(2)}) collective-permute-start(bf16[512,256]{1,0:T(8,128)(2,1)} %get-tuple-element.16), channel_id=1, source_target_pairs={{0,96},{32,0},{64,32},{96,64},{1,97},{33,1},{65,33},{97,65},{2,98}... | collective-permute-start | bytes 786440 | tf_op jit(solution)/shard_map/ppermute | solution.py:150
  127.0 15.8 %collective-permute-start.54 = (bf16[512,256]{1,0:T(8,128)(2,1)}, bf16[512,256]{1,0:T(8,128)(2,1)}, u32[]{:S(2)}, u32[]{:S(2)}) collective-permute-start(bf16[512,256]{1,0:T(8,128)(2,1)} %get-tuple-element.9), channel_id=1, source_target_pairs={{0,64},{32,96},{64,0},{96,32},{1,65},{33,97},{65,1},{97,33},{2,66}... | collective-permute-start | bytes 786440 | tf_op jit(solution)/shard_map/ppermute | solution.py:150
  128.9 19.0 %collective-permute-start.35 = (bf16[512,256]{1,0:T(8,128)(2,1)}, bf16[512,256]{1,0:T(8,128)(2,1)}, u32[]{:S(2)}, u32[]{:S(2)}) collective-permute-start(bf16[512,256]{1,0:T(8,128)(2,1)} %get-tuple-element.14), channel_id=1, source_target_pairs={{0,32},{32,64},{64,96},{96,0},{1,33},{33,65},{65,97},{97,1},{2,34}... | collective-permute-start | bytes 786440 | tf_op jit(solution)/shard_map/ppermute | solution.py:150
  147.9 24.9 %collective-permute-start.28 = (bf16[2,4,2,64,256]{4,3,2,1,0:T(8,128)(2,1)S(1)}, bf16[2,4,2,64,256]{4,3,2,1,0:T(8,128)(2,1)S(1)}, u32[]{:S(2)}, u32[]{:S(2)}) collective-permute-start(bf16[2,4,2,64,256]{4,3,2,1,0:T(8,128)(2,1)S(1)} %get-tuple-element.36.refs_2_), channel_id=1, source_target_pairs={{0,32},{32,64},{64,96},{96,0},{1,33},{33,65},{65,97},{97,1},{2,34}... | collective-permute-start | bytes 1572872 | tf_op jit(solution)/shard_map/ppermute | solution.py:150
  150.9 25.0 %collective-permute-start.29 = (bf16[2,4,2,64,256]{4,3,2,1,0:T(8,128)(2,1)S(1)}, bf16[2,4,2,64,256]{4,3,2,1,0:T(8,128)(2,1)S(1)}, u32[]{:S(2)}, u32[]{:S(2)}) collective-permute-start(bf16[2,4,2,64,256]{4,3,2,1,0:T(8,128)(2,1)S(1)} %get-tuple-element.36.refs_2_), channel_id=1, source_target_pairs={{0,96},{32,0},{64,32},{96,64},{1,97},{33,1},{65,33},{97,65},{2,98}... | collective-permute-start | bytes 1572872 | tf_op jit(solution)/shard_map/ppermute | solution.py:150
  172.8 70.9 %collective-permute-start.42 = (f32[2,512,384]{2,1,0:T(8,128)}, f32[2,512,384]{2,1,0:T(8,128)}, u32[]{:S(2)}, u32[]{:S(2)}) collective-permute-start(f32[2,512,384]{2,1,0:T(8,128)} %shard_map.46), channel_id=1, source_target_pairs={{0,16},{16,0},{1,17},{17,1},{2,18},{18,2},{3,19},{19,3},{4,20},{20... | collective-permute-start | bytes 4718600 | tf_op jit(solution)/shard_map/ppermute | solution.py:150
  176.7 16.7 %collective-permute-start.37 = (bf16[512,256]{1,0:T(8,128)(2,1)}, bf16[512,256]{1,0:T(8,128)(2,1)}, u32[]{:S(2)}, u32[]{:S(2)}) collective-permute-start(bf16[512,256]{1,0:T(8,128)(2,1)} %get-tuple-element.12), channel_id=1, source_target_pairs={{0,64},{32,96},{64,0},{96,32},{1,65},{33,97},{65,1},{97,33},{2,66}... | collective-permute-start | bytes 786440 | tf_op jit(solution)/shard_map/ppermute | solution.py:150
  178.7 15.1 %collective-permute-start.30 = (bf16[1,4,2,64,256]{4,3,2,1,0:T(8,128)(2,1)S(1)}, bf16[1,4,2,64,256]{4,3,2,1,0:T(8,128)(2,1)S(1)}, u32[]{:S(2)}, u32[]{:S(2)}) collective-permute-start(bf16[1,4,2,64,256]{4,3,2,1,0:T(8,128)(2,1)S(1)} %slice.54), channel_id=1, source_target_pairs={{0,32},{32,64},{64,96},{96,0},{1,33},{33,65},{65,97},{97,1},{2,34}... | collective-permute-start | bytes 786440 | tf_op jit(solution)/shard_map/ppermute | solution.py:150
  183.3 15.3 %collective-permute-start.31 = (bf16[1,4,2,64,256]{4,3,2,1,0:T(8,128)(2,1)S(1)}, bf16[1,4,2,64,256]{4,3,2,1,0:T(8,128)(2,1)S(1)}, u32[]{:S(2)}, u32[]{:S(2)}) collective-permute-start(bf16[1,4,2,64,256]{4,3,2,1,0:T(8,128)(2,1)S(1)} %slice.55), channel_id=1, source_target_pairs={{0,96},{32,0},{64,32},{96,64},{1,97},{33,1},{65,33},{97,65},{2,98}... | collective-permute-start | bytes 786440 | tf_op jit(solution)/shard_map/ppermute | solution.py:150
  193.4 45.2 %collective-permute-start.55 = (f32[2,512,256]{2,1,0:T(8,128)S(1)}, f32[2,512,256]{2,1,0:T(8,128)S(1)}, u32[]{:S(2)}, u32[]{:S(2)}) collective-permute-start(f32[2,512,256]{2,1,0:T(8,128)S(1)} %shard_map.49), channel_id=1, source_target_pairs={{0,16},{16,0},{1,17},{17,1},{2,18},{18,2},{3,19},{19,3},{4,20},{20... | collective-permute-start | bytes 3145736 | tf_op jit(solution)/shard_map/ppermute | solution.py:150
  198.5 21.2 %collective-permute-start.39 = (bf16[512,384]{1,0:T(8,128)(2,1)S(1)}, bf16[512,384]{1,0:T(8,128)(2,1)S(1)}, u32[]{:S(2)}, u32[]{:S(2)}) collective-permute-start(bf16[512,384]{1,0:T(8,128)(2,1)S(1)} %get-tuple-element.27), channel_id=1, source_target_pairs={{0,32},{32,64},{64,96},{96,0},{1,33},{33,65},{65,97},{97,1},{2,34}... | collective-permute-start | bytes 1179656 | tf_op jit(solution)/shard_map/ppermute | solution.py:150
  205.0 47.3 %collective-permute-start.38 = (f32[2,512,256]{2,1,0:T(8,128)S(1)}, f32[2,512,256]{2,1,0:T(8,128)S(1)}, u32[]{:S(2)}, u32[]{:S(2)}) collective-permute-start(f32[2,512,256]{2,1,0:T(8,128)S(1)} %shard_map.47), channel_id=1, source_target_pairs={{0,16},{16,0},{1,17},{17,1},{2,18},{18,2},{3,19},{19,3},{4,20},{20... | collective-permute-start | bytes 3145736 | tf_op jit(solution)/shard_map/ppermute | solution.py:150
  217.3 17.6 %collective-permute-start.40 = (bf16[512,384]{1,0:T(8,128)(2,1)S(1)}, bf16[512,384]{1,0:T(8,128)(2,1)S(1)}, u32[]{:S(2)}, u32[]{:S(2)}) collective-permute-start(bf16[512,384]{1,0:T(8,128)(2,1)S(1)} %get-tuple-element.26), channel_id=1, source_target_pairs={{0,96},{32,0},{64,32},{96,64},{1,97},{33,1},{65,33},{97,65},{2,98}... | collective-permute-start | bytes 1179656 | tf_op jit(solution)/shard_map/ppermute | solution.py:150
  219.8 15.2 %collective-permute-start.41 = (bf16[512,384]{1,0:T(8,128)(2,1)S(1)}, bf16[512,384]{1,0:T(8,128)(2,1)S(1)}, u32[]{:S(2)}, u32[]{:S(2)}) collective-permute-start(bf16[512,384]{1,0:T(8,128)(2,1)S(1)} %get-tuple-element.25), channel_id=1, source_target_pairs={{0,64},{32,96},{64,0},{96,32},{1,65},{33,97},{65,1},{97,33},{2,66}... | collective-permute-start | bytes 1179656 | tf_op jit(solution)/shard_map/ppermute | solution.py:150
  234.9 13.9 %collective-permute-start.33 = (bf16[512,256]{1,0:T(8,128)(2,1)S(1)}, bf16[512,256]{1,0:T(8,128)(2,1)S(1)}, u32[]{:S(2)}, u32[]{:S(2)}) collective-permute-start(bf16[512,256]{1,0:T(8,128)(2,1)S(1)} %get-tuple-element.22), channel_id=1, source_target_pairs={{0,96},{32,0},{64,32},{96,64},{1,97},{33,1},{65,33},{97,65},{2,98}... | collective-permute-start | bytes 786440 | tf_op jit(solution)/shard_map/ppermute | solution.py:150
  (72 other events, 738.7 us)

commit v3 on v2

--- a/solution.py
+++ b/solution.py
@@ -101,7 +101,7 @@
     return numerator, denominator
 
 
-def compute_kernel(layout, at, merging, at_ref, *refs):
+def compute_kernel(layout, at, merging, at_ref, *refs, done=None):
     a_refs, refs = refs[:2], refs[2:]
     count = 1 + max(n for pair in layout for n, _ in pair)
     arrays, refs = refs[:count], refs[count:]
@@ -117,13 +117,31 @@
             out_ref[0, tile] = numerator
             out_ref[1, tile] = denominator
             continue
-        other_ref, earlier = refs[0], refs[1:-1]
+        other_ref = refs[0]
         merged = (numerator + other_ref[0, tile]) / (denominator + other_ref[1, tile])
-        column = 0
-        for ref in earlier:
-            out_ref[tile, column:column + ref.shape[1]] = ref[tile]
-            column += ref.shape[1]
-        out_ref[tile, column:column + width] = merged.astype(out_ref.dtype)
+        out_ref[tile] = merged.astype(out_ref.dtype)
+        if done is not None:
+            done(tile)
+
+
+def last_kernel(layout, at, at_ref, *refs):
+    refs, (out_ref, merged_ref, sems) = refs[:-3], refs[-3:]
+    refs, earlier = refs[:-2], refs[-2:]
+    copies, column = [], 0
+    for n, ref in enumerate(earlier):
+        part = out_ref.at[:, column:column + ref.shape[1]]
+        copies.append(pltpu.make_async_copy(ref, part, sems.at[n]))
+        copies[-1].start()
+        column += ref.shape[1]
+
+    def done(tile):
+        part = out_ref.at[tile, column:column + merged_ref.shape[1]]
+        copies.append(pltpu.make_async_copy(merged_ref.at[tile], part, sems.at[len(copies)]))
+        copies[-1].start()
+
+    compute_kernel(layout, at, True, at_ref, *refs, merged_ref, done=done)
+    for copy in copies:
+        copy.wait()
 
 
 def partial_sums(here, a, grads, ws, at):
@@ -138,12 +156,24 @@
 def merge(here, a, grads, ws, at, other, earlier):
     layout, cs = grads
     rows, cols = ws[0].shape[0], cs[0].shape[-1]
+    arrays = [*a, *cs, *ws, other, *earlier]
     width = cols + sum(e.shape[1] for e in earlier)
-    return in_vmem(
-        functools.partial(compute_kernel, layout, at, True), here,
-        [*a, *cs, *ws, other, *earlier],
-        jax.ShapeDtypeStruct((rows, width), jnp.bfloat16),
-    )
+    out = jax.ShapeDtypeStruct((rows, width), jnp.bfloat16)
+    if not earlier:
+        return in_vmem(functools.partial(compute_kernel, layout, at, True), here, arrays, out)
+    return pl.pallas_call(
+        functools.partial(last_kernel, layout, at),
+        out_shape=out,
+        in_specs=[pl.BlockSpec(memory_space=pltpu.SMEM)]
+        + [pl.BlockSpec(memory_space=pltpu.VMEM) for _ in arrays],
+        out_specs=pl.BlockSpec(memory_space=pltpu.HBM),
+        scratch_shapes=[
+            pltpu.VMEM((rows, cols), out.dtype),
+            pltpu.SemaphoreType.DMA((len(earlier) + rows // RTILE,)),
+        ],
+        compiler_params=pltpu.CompilerParams(vmem_limit_bytes=VMEM_LIMIT),
+        name="merge",
+    )(here, *arrays)
 
 
 def send(axis, size, step, value):

time: 257 us -> 257 us (level)
    pallas_call x6 -> x5, Pallas kernels: 26.6 us -> 22.5 us  [in_vmem(): pl.pallas_call(kernel, out_shape=out_shape, in_specs=[pl.BlockSpec(memory...]
    pallas_call x0 -> x1, Pallas kernels: none -> 3.8 us  [merge(): pl.pallas_call(functools.partial(last_kernel, layout, at), out_shape=out,...]
where the time goes in v3:
time: 257 us; the launch traced here: 256 us
  waiting for transfers between devices  97.9 us (38%)
  starting transfers between devices  96.7 us (38%)
  Pallas kernels  33 us (13%)
  local copies, waits for them, and re-layouts  24.9 us (10%)
  other arithmetic  2.96 us (1%)
    ppermute x56, waiting for transfers between devices, send(): lax.ppermute(value, axis, [(i, (i + step) % size) for i in range(size)])  97.9 us
    ppermute x56, starting transfers between devices, send(): lax.ppermute(value, axis, [(i, (i + step) % size) for i in range(size)])  88.5 us
    pallas_call x5, Pallas kernels, in_vmem(): pl.pallas_call(kernel, out_shape=out_shape, in_specs=[pl.BlockSpec(memory...  22.5 us
    unnamed x95, local copies, waits for them, and re-layouts  11.2 us
    dynamic_slice x4, local copies, waits for them, and re-layouts, piece(): return lax.dynamic_slice(source, (base, start), (rows, width))  8.34 us
    all_to_all x2, starting transfers between devices, columns_for(): moved = lax.all_to_all(cut, fsdp, split_axis=1, concat_axis=0, tiled=True)  8.19 us
    pallas_call x2, Pallas kernels, transposed(): pl.pallas_call(transpose_kernel, out_shape=jax.ShapeDtypeStruct((m, r, Z...  6.64 us
  transfers between devices with their start and end apart: 58, of which 22 were waited for; matrix products, arithmetic and copies ran while one was open for 7% of the time, Pallas kernels for 10%

profile of v3, /device:TPU:0, one launch (start us, length us, event | category | flops | bytes accessed | tf_op | source)
XLA Modules:
  0.0 256.3 jit_solution(1444866503394750423)
XLA Ops:
  9.4 2.8 %collective-permute-done.2 = bf16[64,1024]{1,0:T(8,128)(2,1)S(1)} collective-permute-done((bf16[64,1024]{1,0:T(8,128)(2,1)S(1)}, bf16[64,1024]{1,0:T(8,128)(2,1)S(1)}, u32[]{:S(2)}, u32[]{:S(2)}) %collective-permute-start.2) | collective-permute-done | bytes 131104 | tf_op jit(solution)/shard_map/ppermute | solution.py:180
  25.5 6.4 %collective-permute-start.17 = (bf16[4,64,512]{2,1,0:T(8,128)(2,1)S(1)}, bf16[4,64,512]{2,1,0:T(8,128)(2,1)S(1)}, u32[]{:S(2)}, u32[]{:S(2)}) collective-permute-start(bf16[4,64,512]{2,1,0:T(8,128)(2,1)S(1)} %collective-permute-done.14.refs_4_), channel_id=1, source_target_pairs={{0,8},{4,12},{8,0},{12,4},{1,9},{5,13},{9,1},{13,5},{2,10},{6,14},... | collective-permute-start | bytes 786440 | tf_op jit(solution)/shard_map/ppermute | solution.py:180
  32.4 3.2 %collective-permute-done.15.refs_5_ = bf16[4,64,512]{2,1,0:T(8,128)(2,1)S(1)} collective-permute-done((bf16[4,64,512]{2,1,0:T(8,128)(2,1)S(1)}, bf16[4,64,512]{2,1,0:T(8,128)(2,1)S(1)}, u32[]{:S(2)}, u32[]{:S(2)}) %collective-permute-start.15) | collective-permute-done | bytes 262176 | tf_op jit(solution)/shard_map/ppermute | solution.py:180
  35.5 4.1 %collective-permute-done.16.refs_6_ = bf16[4,64,512]{2,1,0:T(8,128)(2,1)S(1)} collective-permute-done((bf16[4,64,512]{2,1,0:T(8,128)(2,1)S(1)}, bf16[4,64,512]{2,1,0:T(8,128)(2,1)S(1)}, u32[]{:S(2)}, u32[]{:S(2)}) %collective-permute-start.16) | collective-permute-done | bytes 262176 | tf_op jit(solution)/shard_map/ppermute | solution.py:180
  42.4 3.6 %transpose_acts.3.refs_0_ = bf16[4,512,512]{2,1,0:T(8,128)(2,1)} custom-call(s32[3]{0:T(128)S(1)} %pad_add_fusion.at_ref, bf16[4,64,512]{2,1,0:T(8,128)(2,1)} %copy-done.33, bf16[4,64,512]{2,1,0:T(8,128)(2,1)} %copy-done.39, bf16[4,64,512]{2,1,0:T(8,128)(2,1)} %copy-done.40, bf16[4,64,512]{2,1,0:T(8,128)(2,1)} %copy-done.42, bf16[4,64,512]{2,1,0:T(8,128)(2,1)} %copy-done.38, ...), custom_call_target="tpu_custom_call" | custom-call | tf_op jit(solution)/shard_map/transpose_acts/pallas_call | solution.py:65
  47.5 3.9 %all-to-all-start = ((bf16[64,16,384]{2,0,1:T(8,128)(2,1)}), bf16[64,16,384]{2,0,1:T(8,128)(2,1)S(1)}, u32[]{:S(2)}, u32[]{:S(2)}) async-start(bf16[64,16,384]{2,0,1:T(8,128)(2,1)} %copy.7), calls=%async_computation | async-start | bytes 1572864 | tf_op jit(solution)/shard_map/all_to_all | solution.py:226
  57.4 2.9 %collective-permute-start.26 = (bf16[512,384]{1,0:T(8,128)(2,1)S(1)}, bf16[512,384]{1,0:T(8,128)(2,1)S(1)}, u32[]{:S(2)}, u32[]{:S(2)}) collective-permute-start(bf16[512,384]{1,0:T(8,128)(2,1)S(1)} %get-tuple-element.30), channel_id=1, source_target_pairs={{0,96},{32,0},{64,32},{96,64},{1,97},{33,1},{65,33},{97,65},{2,98}... | collective-permute-start | bytes 1179656 | tf_op jit(solution)/shard_map/ppermute | solution.py:180
  60.3 8.2 %collective-permute-done.6.refs_4_ = bf16[4,64,512]{2,1,0:T(8,128)(2,1)S(1)} collective-permute-done((bf16[4,64,512]{2,1,0:T(8,128)(2,1)S(1)}, bf16[4,64,512]{2,1,0:T(8,128)(2,1)S(1)}, u32[]{:S(2)}, u32[]{:S(2)}) %collective-permute-start.6) | collective-permute-done | bytes 262176 | tf_op jit(solution)/shard_map/ppermute | solution.py:180
  72.2 10.0 %collective-permute-done.4.refs_2_ = bf16[4,64,512]{2,1,0:T(8,128)(2,1)S(1)} collective-permute-done((bf16[4,64,512]{2,1,0:T(8,128)(2,1)S(1)}, bf16[4,64,512]{2,1,0:T(8,128)(2,1)S(1)}, u32[]{:S(2)}, u32[]{:S(2)}) %collective-permute-start.4) | collective-permute-done | bytes 262176 | tf_op jit(solution)/shard_map/ppermute | solution.py:180
  90.8 4.3 %all-to-all-start.1 = ((bf16[64,16,512]{2,0,1:T(8,128)(2,1)}), bf16[64,16,512]{2,0,1:T(8,128)(2,1)}, u32[]{:S(2)}, u32[]{:S(2)}) async-start(bf16[64,16,512]{2,0,1:T(8,128)(2,1)} %copy.8), calls=%async_computation.1 | async-start | bytes 2097152 | tf_op jit(solution)/shard_map/all_to_all | solution.py:226
  99.7 3.0 %transpose_acts.2.refs_0_ = bf16[4,512,512]{2,1,0:T(8,128)(2,1)S(1)} custom-call(s32[3]{0:T(128)S(1)} %pad_add_fusion.at_ref, bf16[4,64,512]{2,1,0:T(8,128)(2,1)} %copy-done.32, bf16[4,64,512]{2,1,0:T(8,128)(2,1)} %copy-done.35, bf16[4,64,512]{2,1,0:T(8,128)(2,1)} %copy-done.36, bf16[4,64,512]{2,1,0:T(8,128)(2,1)} %copy-done.37, ...), custom_call_target="tpu_custom_call" | custom-call | tf_op jit(solution)/shard_map/transpose_acts/pallas_call | solution.py:65
  103.0 5.5 %collective-permute-done.19.refs_3_ = bf16[1,4,2,64,384]{4,3,2,1,0:T(8,128)(2,1)S(1)} collective-permute-done((bf16[1,4,2,64,384]{4,3,2,1,0:T(8,128)(2,1)S(1)}, bf16[1,4,2,64,384]{4,3,2,1,0:T(8,128)(2,1)S(1)}, u32[]{:S(2)}, u32[]{:S(2)}) %collective-permute-start.19) | collective-permute-done | bytes 393248 | tf_op jit(solution)/shard_map/ppermute | solution.py:180
  110.6 6.4 %collective-permute-done.20.refs_4_ = bf16[1,4,2,64,384]{4,3,2,1,0:T(8,128)(2,1)S(1)} collective-permute-done((bf16[1,4,2,64,384]{4,3,2,1,0:T(8,128)(2,1)S(1)}, bf16[1,4,2,64,384]{4,3,2,1,0:T(8,128)(2,1)S(1)}, u32[]{:S(2)}, u32[]{:S(2)}) %collective-permute-start.20) | collective-permute-done | bytes 393248 | tf_op jit(solution)/shard_map/ppermute | solution.py:180
  118.6 2.9 %dynamic-slice_bitcast_fusion.4 = (bf16[512,256]{1,0:T(8,128)(2,1)}, bf16[512,256]{1,0:T(8,128)(2,1)}, bf16[512,256]{1,0:T(8,128)(2,1)}, bf16[512,256]{1,0:T(8,1...) fusion(bf16[1,4096,896]{2,1,0:T(8,128)(2,1)} %param.4, ...), kind=kLoop, calls=%fused_computation.5 | loop fusion | bytes 4194320 | tf_op jit(solution)/shard_map/dynamic_slice | solution.py:220
  121.9 3.5 %collective-permute-done.23.refs_7_ = bf16[1,4,2,64,384]{4,3,2,1,0:T(8,128)(2,1)S(1)} collective-permute-done((bf16[1,4,2,64,384]{4,3,2,1,0:T(8,128)(2,1)S(1)}, bf16[1,4,2,64,384]{4,3,2,1,0:T(8,128)(2,1)S(1)}, u32[]{:S(2)}, u32[]{:S(2)}) %collective-permute-start.23) | collective-permute-done | bytes 393248 | tf_op jit(solution)/shard_map/ppermute | solution.py:180
  130.4 6.3 %shard_map.46 = f32[2,512,384]{2,1,0:T(8,128)} custom-call(s32[3]{0:T(128)S(1)} %pad_add_fusion.at_ref, bf16[4,512,512]{2,1,0:T(8,128)(2,1)} %transpose_acts.3.refs_0_, bf16[4,512,512]{2,1,0:T(8,128)(2,1)} %collective-permute-done.18.refs_1_, bf16[2,4,2,64,384]{4,3,2,1,0:T(8,128)(2,1)S(1)} %bitcast.55, ...), custom_call_target="tpu_custom_call" | custom-call | tf_op jit(solution)/shard_map/pallas_call | solution.py:25
  142.8 2.9 %collective-permute-start.46 = (bf16[1,4,2,64,256]{4,3,2,1,0:T(8,128)(2,1)S(1)}, bf16[1,4,2,64,256]{4,3,2,1,0:T(8,128)(2,1)}, u32[]{:S(2)}, u32[]{:S(2)}) collective-permute-start(bf16[1,4,2,64,256]{4,3,2,1,0:T(8,128)(2,1)S(1)} %get-tuple-element.33), channel_id=1, source_target_pairs={{0,96},{32,0},{64,32},{96,64},{1,97},{33,1},{65,33},{97,65},{2,98}... | collective-permute-start | bytes 786440 | tf_op jit(solution)/shard_map/ppermute | solution.py:180
  158.6 8.3 %collective-permute-done.44.refs_4_ = bf16[1,4,2,64,256]{4,3,2,1,0:T(8,128)(2,1)S(1)} collective-permute-done((bf16[1,4,2,64,256]{4,3,2,1,0:T(8,128)(2,1)S(1)}, bf16[1,4,2,64,256]{4,3,2,1,0:T(8,128)(2,1)S(1)}, u32[]{:S(2)}, u32[]{:S(2)}) %collective-permute-start.44) | collective-permute-done | bytes 262176 | tf_op jit(solution)/shard_map/ppermute | solution.py:180
  169.8 3.0 %collective-permute-start.48 = (bf16[1,4,2,64,256]{4,3,2,1,0:T(8,128)(2,1)}, bf16[1,4,2,64,256]{4,3,2,1,0:T(8,128)(2,1)}, u32[]{:S(2)}, u32[]{:S(2)}) collective-permute-start(bf16[1,4,2,64,256]{4,3,2,1,0:T(8,128)(2,1)} %collective-permute-done.46.refs_6_), channel_id=1, source_target_pairs={{0,96},{32,0},{64,32},{96,64},{1,97},{33,1},{65,33},{97,65},{2,98}... | collective-permute-start | bytes 786440 | tf_op jit(solution)/shard_map/ppermute | solution.py:180
  172.8 3.1 %collective-permute-start.42 = (f32[2,512,384]{2,1,0:T(8,128)}, f32[2,512,384]{2,1,0:T(8,128)}, u32[]{:S(2)}, u32[]{:S(2)}) collective-permute-start(f32[2,512,384]{2,1,0:T(8,128)} %shard_map.46), channel_id=1, source_target_pairs={{0,16},{16,0},{1,17},{17,1},{2,18},{18,2},{3,19},{19,3},{4,20},{20... | collective-permute-start | bytes 4718600 | tf_op jit(solution)/shard_map/ppermute | solution.py:180
  179.7 3.6 %collective-permute-done.48.refs_8_ = bf16[1,4,2,64,256]{4,3,2,1,0:T(8,128)(2,1)} collective-permute-done((bf16[1,4,2,64,256]{4,3,2,1,0:T(8,128)(2,1)}, bf16[1,4,2,64,256]{4,3,2,1,0:T(8,128)(2,1)}, u32[]{:S(2)}, u32[]{:S(2)}) %collective-permute-start.48) | collective-permute-done | bytes 262176 | tf_op jit(solution)/shard_map/ppermute | solution.py:180
  183.3 4.3 %collective-permute-start.31 = (bf16[1,4,2,64,256]{4,3,2,1,0:T(8,128)(2,1)S(1)}, bf16[1,4,2,64,256]{4,3,2,1,0:T(8,128)(2,1)S(1)}, u32[]{:S(2)}, u32[]{:S(2)}) collective-permute-start(bf16[1,4,2,64,256]{4,3,2,1,0:T(8,128)(2,1)S(1)} %slice.55), channel_id=1, source_target_pairs={{0,96},{32,0},{64,32},{96,64},{1,97},{33,1},{65,33},{97,65},{2,98}... | collective-permute-start | bytes 786440 | tf_op jit(solution)/shard_map/ppermute | solution.py:180
  189.3 4.0 %shard_map.49 = f32[2,512,256]{2,1,0:T(8,128)S(1)} custom-call(s32[3]{0:T(128)S(1)} %pad_add_fusion.at_ref, bf16[4,512,512]{2,1,0:T(8,128)(2,1)} %transpose_acts.3.refs_0_, bf16[4,512,512]{2,1,0:T(8,128)(2,1)} %collective-permute-done.18.refs_1_, bf16[2,4,2,64,256]{4,3,2,1,0:T(8,128)(2,1)S(1)} %copy-done, ...), custom_call_target="tpu_custom_call" | custom-call | tf_op jit(solution)/shard_map/pallas_call | solution.py:25
  193.8 3.2 %collective-permute-start.50 = (bf16[512,256]{1,0:T(8,128)(2,1)S(1)}, bf16[512,256]{1,0:T(8,128)(2,1)S(1)}, u32[]{:S(2)}, u32[]{:S(2)}) collective-permute-start(bf16[512,256]{1,0:T(8,128)(2,1)S(1)} %get-tuple-element.18), channel_id=1, source_target_pairs={{0,96},{32,0},{64,32},{96,64},{1,97},{33,1},{65,33},{97,65},{2,98}... | collective-permute-start | bytes 786440 | tf_op jit(solution)/shard_map/ppermute | solution.py:180
  198.7 3.7 %shard_map.47 = f32[2,512,256]{2,1,0:T(8,128)S(1)} custom-call(s32[3]{0:T(128)S(1)} %pad_add_fusion.at_ref, bf16[4,512,512]{2,1,0:T(8,128)(2,1)} %transpose_acts.3.refs_0_, bf16[4,512,512]{2,1,0:T(8,128)(2,1)} %collective-permute-done.18.refs_1_, bf16[2,4,2,64,256]{4,3,2,1,0:T(8,128)(2,1)S(1)} %get-tuple-element.36.refs_2_, ...), custom_call_target="tpu_custom_call" | custom-call | tf_op jit(solution)/shard_map/pallas_call | solution.py:25
  207.6 9.7 %collective-permute-done.51.refs_12_ = bf16[512,256]{1,0:T(8,128)(2,1)S(1)} collective-permute-done((bf16[512,256]{1,0:T(8,128)(2,1)S(1)}, bf16[512,256]{1,0:T(8,128)(2,1)S(1)}, u32[]{:S(2)}, u32[]{:S(2)}) %collective-permute-start.51) | collective-permute-done | bytes 262176 | tf_op jit(solution)/shard_map/ppermute | solution.py:180
  219.8 15.2 %collective-permute-done.40.refs_11_ = bf16[512,384]{1,0:T(8,128)(2,1)S(1)} collective-permute-done((bf16[512,384]{1,0:T(8,128)(2,1)S(1)}, bf16[512,384]{1,0:T(8,128)(2,1)S(1)}, u32[]{:S(2)}, u32[]{:S(2)}) %collective-permute-start.40) | collective-permute-done | bytes 393248 | tf_op jit(solution)/shard_map/ppermute | solution.py:180
  234.9 3.7 %collective-permute-start.33 = (bf16[512,256]{1,0:T(8,128)(2,1)S(1)}, bf16[512,256]{1,0:T(8,128)(2,1)S(1)}, u32[]{:S(2)}, u32[]{:S(2)}) collective-permute-start(bf16[512,256]{1,0:T(8,128)(2,1)S(1)} %get-tuple-element.22), channel_id=1, source_target_pairs={{0,96},{32,0},{64,32},{96,64},{1,97},{33,1},{65,33},{97,65},{2,98}... | collective-permute-start | bytes 786440 | tf_op jit(solution)/shard_map/ppermute | solution.py:180
  240.2 3.5 %shard_map.50.refs_13_ = bf16[512,256]{1,0:T(8,128)(2,1)S(1)} custom-call(s32[3]{0:T(128)S(1)} %pad_add_fusion.at_ref, bf16[4,512,512]{2,1,0:T(8,128)(2,1)S(1)} %transpose_acts.2.refs_0_, bf16[4,512,512]{2,1,0:T(8,128)(2,1)} %collective-permute-done.10.refs_1_, bf16[2,4,2,64,256]{4,3,2,1,0:T(8,128)(2,1)S(1)} %copy-done, ...), custom_call_target="tpu_custom_call" | custom-call | tf_op jit(solution)/shard_map/pallas_call | solution.py:25
  243.8 5.0 %shard_map.48.refs_12_ = bf16[512,384]{1,0:T(8,128)(2,1)S(1)} custom-call(s32[3]{0:T(128)S(1)} %pad_add_fusion.at_ref, bf16[4,512,512]{2,1,0:T(8,128)(2,1)S(1)} %transpose_acts.2.refs_0_, bf16[4,512,512]{2,1,0:T(8,128)(2,1)} %collective-permute-done.10.refs_1_, bf16[2,4,2,64,384]{4,3,2,1,0:T(8,128)(2,1)S(1)} %bitcast.56, ...), custom_call_target="tpu_custom_call" | custom-call | tf_op jit(solution)/shard_map/pallas_call | solution.py:25
  248.8 3.5 %collective-permute-done.38.refs_11_ = f32[2,512,256]{2,1,0:T(8,128)S(1)} collective-permute-done((f32[2,512,256]{2,1,0:T(8,128)S(1)}, f32[2,512,256]{2,1,0:T(8,128)S(1)}, u32[]{:S(2)}, u32[]{:S(2)}) %collective-permute-start.38) | collective-permute-done | bytes 1048608 | tf_op jit(solution)/shard_map/ppermute | solution.py:180
  252.3 3.8 %merge.1 = bf16[512,896]{1,0:T(8,128)(2,1)} custom-call(s32[3]{0:T(128)S(1)} %pad_add_fusion.at_ref, bf16[4,512,512]{2,1,0:T(8,128)(2,1)S(1)} %transpose_acts.2.refs_0_, bf16[4,512,512]{2,1,0:T(8,128)(2,1)} %collective-permute-done.10.refs_1_, bf16[2,4,2,64,256]{4,3,2,1,0:T(8,128)(2,1)S(1)} %get-tuple-element.36.refs_2_, ...), custom_call_target="tpu_custom_call" | custom-call | tf_op jit(solution)/shard_map/merge/pallas_call | solution.py:164
  (204 shorter events, 97.8 us)
Async XLA Ops:
  16.0 16.0 %collective-permute-start.12 = (bf16[4,64,512]{2,1,0:T(8,128)(2,1)S(1)}, bf16[4,64,512]{2,1,0:T(8,128)(2,1)S(1)}, u32[]{:S(2)}, u32[]{:S(2)}) collective-permute-start(bf16[4,64,512]{2,1,0:T(8,128)(2,1)S(1)} %get-tuple-element.42.refs_0_), channel_id=1, source_target_pairs={{0,12},{4,0},{8,4},{12,8},{1,13},{5,1},{9,5},{13,9},{2,14},{6,2},{... | collective-permute-start | bytes 786440 | tf_op jit(solution)/shard_map/ppermute | solution.py:180
  18.1 14.3 %collective-permute-start.13 = (bf16[4,64,512]{2,1,0:T(8,128)(2,1)S(1)}, bf16[4,64,512]{2,1,0:T(8,128)(2,1)S(1)}, u32[]{:S(2)}, u32[]{:S(2)}) collective-permute-start(bf16[4,64,512]{2,1,0:T(8,128)(2,1)S(1)} %get-tuple-element.42.refs_0_), channel_id=1, source_target_pairs={{0,8},{4,12},{8,0},{12,4},{1,9},{5,13},{9,1},{13,5},{2,10},{6,14},... | collective-permute-start | bytes 786440 | tf_op jit(solution)/shard_map/ppermute | solution.py:180
  20.0 15.6 %collective-permute-start.15 = (bf16[4,64,512]{2,1,0:T(8,128)(2,1)S(1)}, bf16[4,64,512]{2,1,0:T(8,128)(2,1)S(1)}, u32[]{:S(2)}, u32[]{:S(2)}) collective-permute-start(bf16[4,64,512]{2,1,0:T(8,128)(2,1)S(1)} %collective-permute-done.14.refs_4_), channel_id=1, source_target_pairs={{0,4},{4,8},{8,12},{12,0},{1,5},{5,9},{9,13},{13,1},{2,6},{6,10},{... | collective-permute-start | bytes 786440 | tf_op jit(solution)/shard_map/ppermute | solution.py:180
  21.9 17.8 %collective-permute-start.16 = (bf16[4,64,512]{2,1,0:T(8,128)(2,1)S(1)}, bf16[4,64,512]{2,1,0:T(8,128)(2,1)S(1)}, u32[]{:S(2)}, u32[]{:S(2)}) collective-permute-start(bf16[4,64,512]{2,1,0:T(8,128)(2,1)S(1)} %collective-permute-done.14.refs_4_), channel_id=1, source_target_pairs={{0,12},{4,0},{8,4},{12,8},{1,13},{5,1},{9,5},{13,9},{2,14},{6,2},{... | collective-permute-start | bytes 786440 | tf_op jit(solution)/shard_map/ppermute | solution.py:180
  25.5 16.1 %collective-permute-start.17 = (bf16[4,64,512]{2,1,0:T(8,128)(2,1)S(1)}, bf16[4,64,512]{2,1,0:T(8,128)(2,1)S(1)}, u32[]{:S(2)}, u32[]{:S(2)}) collective-permute-start(bf16[4,64,512]{2,1,0:T(8,128)(2,1)S(1)} %collective-permute-done.14.refs_4_), channel_id=1, source_target_pairs={{0,8},{4,12},{8,0},{12,4},{1,9},{5,13},{9,1},{13,5},{2,10},{6,14},... | collective-permute-start | bytes 786440 | tf_op jit(solution)/shard_map/ppermute | solution.py:180
  46.0 82.9 %collective-permute-start.18 = (bf16[4,512,512]{2,1,0:T(8,128)(2,1)}, bf16[4,512,512]{2,1,0:T(8,128)(2,1)}, u32[]{:S(2)}, u32[]{:S(2)}) collective-permute-start(bf16[4,512,512]{2,1,0:T(8,128)(2,1)} %transpose_acts.3.refs_0_), channel_id=1, source_target_pairs={{0,1},{1,0},{2,3},{3,2},{4,5},{5,4},{6,7},{7,6},{8,9},{9,8},{10,11... | collective-permute-start | bytes 6291464 | tf_op jit(solution)/shard_map/ppermute | solution.py:180
  47.5 43.3 %all-to-all-start = ((bf16[64,16,384]{2,0,1:T(8,128)(2,1)}), bf16[64,16,384]{2,0,1:T(8,128)(2,1)S(1)}, u32[]{:S(2)}, u32[]{:S(2)}) async-start(bf16[64,16,384]{2,0,1:T(8,128)(2,1)} %copy.7), calls=%async_computation | async-start | bytes 1572864 | tf_op jit(solution)/shard_map/all_to_all | solution.py:226
  51.4 17.2 %collective-permute-start.6 = (bf16[4,64,512]{2,1,0:T(8,128)(2,1)S(1)}, bf16[4,64,512]{2,1,0:T(8,128)(2,1)S(1)}, u32[]{:S(2)}, u32[]{:S(2)}) collective-permute-start(bf16[4,64,512]{2,1,0:T(8,128)(2,1)S(1)} %get-tuple-element.43.refs_0_), channel_id=1, source_target_pairs={{0,2},{2,0},{1,3},{3,1},{4,6},{6,4},{5,7},{7,5},{8,10},{10,8},{9,1... | collective-permute-start | bytes 786440 | tf_op jit(solution)/shard_map/ppermute | solution.py:180
  53.3 18.0 %collective-permute-start.3 = (bf16[4,64,512]{2,1,0:T(8,128)(2,1)S(1)}, bf16[4,64,512]{2,1,0:T(8,128)(2,1)S(1)}, u32[]{:S(2)}, u32[]{:S(2)}) collective-permute-start(bf16[4,64,512]{2,1,0:T(8,128)(2,1)S(1)} %get-tuple-element.43.refs_0_), channel_id=1, source_target_pairs={{0,4},{4,8},{8,12},{12,0},{1,5},{5,9},{9,13},{13,1},{2,6},{6,10},{... | collective-permute-start | bytes 786440 | tf_op jit(solution)/shard_map/ppermute | solution.py:180
  57.1 27.2 %collective-permute-start.25 = (bf16[512,384]{1,0:T(8,128)(2,1)S(1)}, bf16[512,384]{1,0:T(8,128)(2,1)S(1)}, u32[]{:S(2)}, u32[]{:S(2)}) collective-permute-start(bf16[512,384]{1,0:T(8,128)(2,1)S(1)} %get-tuple-element.31), channel_id=1, source_target_pairs={{0,32},{32,64},{64,96},{96,0},{1,33},{33,65},{65,97},{97,1},{2,34}... | collective-permute-start | bytes 1179656 | tf_op jit(solution)/shard_map/ppermute | solution.py:180
  57.4 29.6 %collective-permute-start.26 = (bf16[512,384]{1,0:T(8,128)(2,1)S(1)}, bf16[512,384]{1,0:T(8,128)(2,1)S(1)}, u32[]{:S(2)}, u32[]{:S(2)}) collective-permute-start(bf16[512,384]{1,0:T(8,128)(2,1)S(1)} %get-tuple-element.30), channel_id=1, source_target_pairs={{0,96},{32,0},{64,32},{96,64},{1,97},{33,1},{65,33},{97,65},{2,98}... | collective-permute-start | bytes 1179656 | tf_op jit(solution)/shard_map/ppermute | solution.py:180
  82.2 20.5 %collective-permute-start.27 = (bf16[512,384]{1,0:T(8,128)(2,1)}, bf16[512,384]{1,0:T(8,128)(2,1)}, u32[]{:S(2)}, u32[]{:S(2)}) collective-permute-start(bf16[512,384]{1,0:T(8,128)(2,1)} %get-tuple-element.29), channel_id=1, source_target_pairs={{0,64},{32,96},{64,0},{96,32},{1,65},{33,97},{65,1},{97,33},{2,66}... | collective-permute-start | bytes 1179656 | tf_op jit(solution)/shard_map/ppermute | solution.py:180
  90.8 48.2 %all-to-all-start.1 = ((bf16[64,16,512]{2,0,1:T(8,128)(2,1)}), bf16[64,16,512]{2,0,1:T(8,128)(2,1)}, u32[]{:S(2)}, u32[]{:S(2)}) async-start(bf16[64,16,512]{2,0,1:T(8,128)(2,1)} %copy.8), calls=%async_computation.1 | async-start | bytes 2097152 | tf_op jit(solution)/shard_map/all_to_all | solution.py:226
  98.8 18.2 %collective-permute-start.20 = (bf16[1,4,2,64,384]{4,3,2,1,0:T(8,128)(2,1)S(1)}, bf16[1,4,2,64,384]{4,3,2,1,0:T(8,128)(2,1)S(1)}, u32[]{:S(2)}, u32[]{:S(2)}) collective-permute-start(bf16[1,4,2,64,384]{4,3,2,1,0:T(8,128)(2,1)S(1)} %bitcast.65), channel_id=1, source_target_pairs={{0,32},{32,64},{64,96},{96,0},{1,33},{33,65},{65,97},{97,1},{2,34}... | collective-permute-start | bytes 1179656 | tf_op jit(solution)/shard_map/ppermute | solution.py:180
  102.8 90.9 %collective-permute-start.10 = (bf16[4,512,512]{2,1,0:T(8,128)(2,1)S(1)}, bf16[4,512,512]{2,1,0:T(8,128)(2,1)}, u32[]{:S(2)}, u32[]{:S(2)}) collective-permute-start(bf16[4,512,512]{2,1,0:T(8,128)(2,1)S(1)} %transpose_acts.2.refs_0_), channel_id=1, source_target_pairs={{0,1},{1,0},{2,3},{3,2},{4,5},{5,4},{6,7},{7,6},{8,9},{9,8},{10,11... | collective-permute-start | bytes 6291464 | tf_op jit(solution)/shard_map/ppermute | solution.py:180
  110.2 15.2 %collective-permute-start.23 = (bf16[1,4,2,64,384]{4,3,2,1,0:T(8,128)(2,1)S(1)}, bf16[1,4,2,64,384]{4,3,2,1,0:T(8,128)(2,1)S(1)}, u32[]{:S(2)}, u32[]{:S(2)}) collective-permute-start(bf16[1,4,2,64,384]{4,3,2,1,0:T(8,128)(2,1)S(1)} %collective-permute-done.19.refs_3_), channel_id=1, source_target_pairs={{0,32},{32,64},{64,96},{96,0},{1,33},{33,65},{65,97},{97,1},{2,34}... | collective-permute-start | bytes 1179656 | tf_op jit(solution)/shard_map/ppermute | solution.py:180
  121.4 18.7 %collective-permute-start.52 = (bf16[512,256]{1,0:T(8,128)(2,1)}, bf16[512,256]{1,0:T(8,128)(2,1)S(1)}, u32[]{:S(2)}, u32[]{:S(2)}) collective-permute-start(bf16[512,256]{1,0:T(8,128)(2,1)} %get-tuple-element.10), channel_id=1, source_target_pairs={{0,32},{32,64},{64,96},{96,0},{1,33},{33,65},{65,97},{97,1},{2,34}... | collective-permute-start | bytes 786440 | tf_op jit(solution)/shard_map/ppermute | solution.py:180
  125.4 17.1 %collective-permute-start.53 = (bf16[512,256]{1,0:T(8,128)(2,1)}, bf16[512,256]{1,0:T(8,128)(2,1)}, u32[]{:S(2)}, u32[]{:S(2)}) collective-permute-start(bf16[512,256]{1,0:T(8,128)(2,1)} %get-tuple-element.16), channel_id=1, source_target_pairs={{0,96},{32,0},{64,32},{96,64},{1,97},{33,1},{65,33},{97,65},{2,98}... | collective-permute-start | bytes 786440 | tf_op jit(solution)/shard_map/ppermute | solution.py:180
  127.0 15.8 %collective-permute-start.54 = (bf16[512,256]{1,0:T(8,128)(2,1)}, bf16[512,256]{1,0:T(8,128)(2,1)}, u32[]{:S(2)}, u32[]{:S(2)}) collective-permute-start(bf16[512,256]{1,0:T(8,128)(2,1)} %get-tuple-element.9), channel_id=1, source_target_pairs={{0,64},{32,96},{64,0},{96,32},{1,65},{33,97},{65,1},{97,33},{2,66}... | collective-permute-start | bytes 786440 | tf_op jit(solution)/shard_map/ppermute | solution.py:180
  128.9 19.0 %collective-permute-start.35 = (bf16[512,256]{1,0:T(8,128)(2,1)}, bf16[512,256]{1,0:T(8,128)(2,1)}, u32[]{:S(2)}, u32[]{:S(2)}) collective-permute-start(bf16[512,256]{1,0:T(8,128)(2,1)} %get-tuple-element.14), channel_id=1, source_target_pairs={{0,32},{32,64},{64,96},{96,0},{1,33},{33,65},{65,97},{97,1},{2,34}... | collective-permute-start | bytes 786440 | tf_op jit(solution)/shard_map/ppermute | solution.py:180
  147.9 24.9 %collective-permute-start.28 = (bf16[2,4,2,64,256]{4,3,2,1,0:T(8,128)(2,1)S(1)}, bf16[2,4,2,64,256]{4,3,2,1,0:T(8,128)(2,1)S(1)}, u32[]{:S(2)}, u32[]{:S(2)}) collective-permute-start(bf16[2,4,2,64,256]{4,3,2,1,0:T(8,128)(2,1)S(1)} %get-tuple-element.36.refs_2_), channel_id=1, source_target_pairs={{0,32},{32,64},{64,96},{96,0},{1,33},{33,65},{65,97},{97,1},{2,34}... | collective-permute-start | bytes 1572872 | tf_op jit(solution)/shard_map/ppermute | solution.py:180
  150.9 25.0 %collective-permute-start.29 = (bf16[2,4,2,64,256]{4,3,2,1,0:T(8,128)(2,1)S(1)}, bf16[2,4,2,64,256]{4,3,2,1,0:T(8,128)(2,1)S(1)}, u32[]{:S(2)}, u32[]{:S(2)}) collective-permute-start(bf16[2,4,2,64,256]{4,3,2,1,0:T(8,128)(2,1)S(1)} %get-tuple-element.36.refs_2_), channel_id=1, source_target_pairs={{0,96},{32,0},{64,32},{96,64},{1,97},{33,1},{65,33},{97,65},{2,98}... | collective-permute-start | bytes 1572872 | tf_op jit(solution)/shard_map/ppermute | solution.py:180
  172.8 70.9 %collective-permute-start.42 = (f32[2,512,384]{2,1,0:T(8,128)}, f32[2,512,384]{2,1,0:T(8,128)}, u32[]{:S(2)}, u32[]{:S(2)}) collective-permute-start(f32[2,512,384]{2,1,0:T(8,128)} %shard_map.46), channel_id=1, source_target_pairs={{0,16},{16,0},{1,17},{17,1},{2,18},{18,2},{3,19},{19,3},{4,20},{20... | collective-permute-start | bytes 4718600 | tf_op jit(solution)/shard_map/ppermute | solution.py:180
  176.7 16.7 %collective-permute-start.37 = (bf16[512,256]{1,0:T(8,128)(2,1)}, bf16[512,256]{1,0:T(8,128)(2,1)}, u32[]{:S(2)}, u32[]{:S(2)}) collective-permute-start(bf16[512,256]{1,0:T(8,128)(2,1)} %get-tuple-element.12), channel_id=1, source_target_pairs={{0,64},{32,96},{64,0},{96,32},{1,65},{33,97},{65,1},{97,33},{2,66}... | collective-permute-start | bytes 786440 | tf_op jit(solution)/shard_map/ppermute | solution.py:180
  178.7 15.1 %collective-permute-start.30 = (bf16[1,4,2,64,256]{4,3,2,1,0:T(8,128)(2,1)S(1)}, bf16[1,4,2,64,256]{4,3,2,1,0:T(8,128)(2,1)S(1)}, u32[]{:S(2)}, u32[]{:S(2)}) collective-permute-start(bf16[1,4,2,64,256]{4,3,2,1,0:T(8,128)(2,1)S(1)} %slice.54), channel_id=1, source_target_pairs={{0,32},{32,64},{64,96},{96,0},{1,33},{33,65},{65,97},{97,1},{2,34}... | collective-permute-start | bytes 786440 | tf_op jit(solution)/shard_map/ppermute | solution.py:180
  183.3 15.3 %collective-permute-start.31 = (bf16[1,4,2,64,256]{4,3,2,1,0:T(8,128)(2,1)S(1)}, bf16[1,4,2,64,256]{4,3,2,1,0:T(8,128)(2,1)S(1)}, u32[]{:S(2)}, u32[]{:S(2)}) collective-permute-start(bf16[1,4,2,64,256]{4,3,2,1,0:T(8,128)(2,1)S(1)} %slice.55), channel_id=1, source_target_pairs={{0,96},{32,0},{64,32},{96,64},{1,97},{33,1},{65,33},{97,65},{2,98}... | collective-permute-start | bytes 786440 | tf_op jit(solution)/shard_map/ppermute | solution.py:180
  193.4 45.2 %collective-permute-start.55 = (f32[2,512,256]{2,1,0:T(8,128)S(1)}, f32[2,512,256]{2,1,0:T(8,128)S(1)}, u32[]{:S(2)}, u32[]{:S(2)}) collective-permute-start(f32[2,512,256]{2,1,0:T(8,128)S(1)} %shard_map.49), channel_id=1, source_target_pairs={{0,16},{16,0},{1,17},{17,1},{2,18},{18,2},{3,19},{19,3},{4,20},{20... | collective-permute-start | bytes 3145736 | tf_op jit(solution)/shard_map/ppermute | solution.py:180
  198.5 21.2 %collective-permute-start.39 = (bf16[512,384]{1,0:T(8,128)(2,1)S(1)}, bf16[512,384]{1,0:T(8,128)(2,1)S(1)}, u32[]{:S(2)}, u32[]{:S(2)}) collective-permute-start(bf16[512,384]{1,0:T(8,128)(2,1)S(1)} %get-tuple-element.27), channel_id=1, source_target_pairs={{0,32},{32,64},{64,96},{96,0},{1,33},{33,65},{65,97},{97,1},{2,34}... | collective-permute-start | bytes 1179656 | tf_op jit(solution)/shard_map/ppermute | solution.py:180
  205.0 47.3 %collective-permute-start.38 = (f32[2,512,256]{2,1,0:T(8,128)S(1)}, f32[2,512,256]{2,1,0:T(8,128)S(1)}, u32[]{:S(2)}, u32[]{:S(2)}) collective-permute-start(f32[2,512,256]{2,1,0:T(8,128)S(1)} %shard_map.47), channel_id=1, source_target_pairs={{0,16},{16,0},{1,17},{17,1},{2,18},{18,2},{3,19},{19,3},{4,20},{20... | collective-permute-start | bytes 3145736 | tf_op jit(solution)/shard_map/ppermute | solution.py:180
  217.3 17.6 %collective-permute-start.40 = (bf16[512,384]{1,0:T(8,128)(2,1)S(1)}, bf16[512,384]{1,0:T(8,128)(2,1)S(1)}, u32[]{:S(2)}, u32[]{:S(2)}) collective-permute-start(bf16[512,384]{1,0:T(8,128)(2,1)S(1)} %get-tuple-element.26), channel_id=1, source_target_pairs={{0,96},{32,0},{64,32},{96,64},{1,97},{33,1},{65,33},{97,65},{2,98}... | collective-permute-start | bytes 1179656 | tf_op jit(solution)/shard_map/ppermute | solution.py:180
  219.8 15.2 %collective-permute-start.41 = (bf16[512,384]{1,0:T(8,128)(2,1)S(1)}, bf16[512,384]{1,0:T(8,128)(2,1)S(1)}, u32[]{:S(2)}, u32[]{:S(2)}) collective-permute-start(bf16[512,384]{1,0:T(8,128)(2,1)S(1)} %get-tuple-element.25), channel_id=1, source_target_pairs={{0,64},{32,96},{64,0},{96,32},{1,65},{33,97},{65,1},{97,33},{2,66}... | collective-permute-start | bytes 1179656 | tf_op jit(solution)/shard_map/ppermute | solution.py:180
  234.9 13.9 %collective-permute-start.33 = (bf16[512,256]{1,0:T(8,128)(2,1)S(1)}, bf16[512,256]{1,0:T(8,128)(2,1)S(1)}, u32[]{:S(2)}, u32[]{:S(2)}) collective-permute-start(bf16[512,256]{1,0:T(8,128)(2,1)S(1)} %get-tuple-element.22), channel_id=1, source_target_pairs={{0,96},{32,0},{64,32},{96,64},{1,97},{33,1},{65,33},{97,65},{2,98}... | collective-permute-start | bytes 786440 | tf_op jit(solution)/shard_map/ppermute | solution.py:180
  (72 other events, 738.7 us)
